TPU v7x, 32 devices: a whole 2x2x4 slice. The times are simulated.
32 devices in a mesh: dp: 2 (over core), seq: 16 (over z, y, x).
Axes of the slice: x: 2, y: 2, z: 4, core: 2. Of those that a mesh axis runs over, the one named last changes fastest.
Arguments:
- block_input: bfloat16 [8192, 1024], P(('dp', 'seq')), may hold values from -6 to 6
- lengths: int32 [2, 2], P('dp'), may hold values from 1 to 1537, 2050 in all within a row
- attn_gain: float32 [1024], replicated, may hold values from 0.5 to 1.5
- w_query: bfloat16 [1024, 1024], replicated, may hold values from -0.1875 to 0.1875
- w_key: bfloat16 [1024, 2048], replicated, may hold values from -0.1875 to 0.1875
- w_value: bfloat16 [1024, 2048], replicated, may hold values from -0.1875 to 0.1875
- w_outgate: bfloat16 [1024, 1024], replicated, may hold values from -0.1875 to 0.1875
- w_beta: bfloat16 [1024, 16], replicated, may hold values from -0.1875 to 0.1875
- w_decay: bfloat16 [1024, 8], replicated, may hold values from -0.1875 to 0.1875
- beta_bias: float32 [16], replicated, may hold values from -3 to 1
- decay_rate: float32 [8], replicated, may hold values from 0.0002 to 0.05
- conv_query: float32 [4, 1024], replicated, may hold values from -3 to 3
- conv_key: float32 [4, 2048], replicated, may hold values from -3 to 3
- conv_value: float32 [4, 2048], replicated, may hold values from -3 to 3
- out_gain: float32 [128], replicated, may hold values from 0.5 to 1.5
- w_out: bfloat16 [1024, 1024], replicated, may hold values from -0.1875 to 0.1875
- mlp_gain: float32 [1024], replicated, may hold values from 0.5 to 1.5
- w_gate: bfloat16 [1024, 2816], replicated, may hold values from -0.1875 to 0.1875
- w_up: bfloat16 [1024, 2816], replicated, may hold values from -0.1875 to 0.1875
- w_down: bfloat16 [2816, 1024], replicated, may hold values from -0.109375 to 0.109375
- out_grad: bfloat16 [8192, 1024], P(('dp', 'seq')), may hold values from -6 to 6
Outputs:
- block_output: bfloat16 [8192, 1024], P(('dp', 'seq'))
- input_grad: bfloat16 [8192, 1024], P(('dp', 'seq'))
- grad_attn_gain: float32 [1024], P(('dp', 'seq'))
- grad_w_query: float32 [1024, 1024], P(('dp', 'seq'))
- grad_w_key: float32 [1024, 2048], P(('dp', 'seq'))
- grad_w_value: float32 [1024, 2048], P(('dp', 'seq'))
- grad_w_outgate: float32 [1024, 1024], P(('dp', 'seq'))
- grad_w_beta: float32 [1024, 16], P(('dp', 'seq'))
- grad_w_decay: float32 [1024, 8], P(('dp', 'seq'))
- grad_beta_bias: float32 [16], replicated
- grad_decay_rate: float32 [8], replicated
- grad_conv_query: float32 [4, 1024], replicated
- grad_conv_key: float32 [4, 2048], replicated
- grad_conv_value: float32 [4, 2048], replicated
- grad_out_gain: float32 [128], replicated
- grad_w_out: float32 [1024, 1024], P(None, ('dp', 'seq'))
- grad_mlp_gain: float32 [1024], P(('dp', 'seq'))
- grad_w_gate: float32 [1024, 2816], P(('dp', 'seq'))
- grad_w_up: float32 [1024, 2816], P(('dp', 'seq'))
- grad_w_down: float32 [2816, 1024], P(None, ('dp', 'seq'))
Inputs may be any that keep to these rules, and one draw needn't show every extreme that they name: `lengths`: row r lists the 2 sequences of group r in packing order; the longest is at most 2560 tokens and every row sums to 2050.
All inputs are finite; a program needn't handle non-finite values.
Results may differ from a plain program's by a relative error of at most 0.022.
Values may be sent and summed in bfloat16 or wider, within the bound.
A program may use at most 512 MiB of HBM per device.

v0:
```python
from functools import partial

import jax
import jax.numpy as jnp
from jax import lax
from jax.experimental import pallas as pl
from jax.experimental.pallas import tpu as pltpu
from jax.sharding import PartitionSpec as P

REFLECTS = 2
KW = 4
BLOCK = 64
SHORTEST = 1024
STEPS = BLOCK * REFLECTS
HALO = 8
RESET_LOG = -80.0
MESH = pl.DeviceIdType.MESH
F32 = jnp.float32
BF16 = jnp.bfloat16
NN = (((1,), (0,)), ((), ()))
NT = (((1,), (1,)), ((), ()))
TN = (((0,), (0,)), ((), ()))
VMEM_LIMIT = 56 * 1024 * 1024
FORWARD_HEADS = 2
BACKWARD_HEADS = 1


def cost(microseconds):
    return pl.CostEstimate(
        flops=int(microseconds * 1e9), bytes_accessed=int(microseconds * 1e6), transcendentals=0
    )


def mm(a, b, dims=NN):
    return lax.dot_general(a.astype(BF16), b.astype(BF16), dims, preferred_element_type=F32)


def halves(a):
    high = a.astype(BF16)
    return high, (a - high.astype(F32)).astype(BF16)


def mm3(a, b):
    ah, al = halves(a)
    bh, bl = halves(b)
    return mm(jnp.concatenate([ah, al], axis=1), jnp.concatenate([bh, bh], axis=0)) + mm(ah, bl)


def mm2(a, b, dims=NN):
    ah, al = halves(a)
    return mm(ah, b, dims) + mm(al, b, dims)


def mm2t(a, b, dims=NN):
    bh, bl = halves(b)
    return mm(a, bh, dims) + mm(a, bl, dims)


def sigmoid(v):
    return 1.0 / (1.0 + jnp.exp(-v))


def step_ids(shape, axis):
    index = lax.broadcasted_iota(jnp.int32, shape, axis)
    return index % BLOCK, index // BLOCK


def step_masks():
    shape = (STEPS, STEPS)
    tm, jm = step_ids(shape, 0)
    tn, jn = step_ids(shape, 1)
    strict = (tm > tn) | ((tm == tn) & (jm > jn))
    size = 4
    first = tm // size == tn // size
    merges = []
    while size < BLOCK:
        merges.append((tm // (2 * size) == tn // (2 * size)) & (tm // size != tn // size))
        size = 2 * size
    eye = ((tm == tn) & (jm == jn)).astype(F32)
    return tm >= tn, strict, first, merges, eye


def unit_lower_inverse(systems, first, merges, eye):
    neg = [jnp.where(first, -a, 0.0) for a in systems]
    inv = [eye + n for n in neg]
    for _ in range(2):
        neg = [mm3(n, n) for n in neg]
        inv = [t + mm3(t, n) for t, n in zip(inv, neg)]
    for merge in merges:
        off = [mm3(jnp.where(merge, a, 0.0), t) for a, t in zip(systems, inv)]
        inv = [t - mm3(t, o) for t, o in zip(inv, off)]
    return inv


def conv_parts(ext_ref, taps, live, columns, rows):
    total = None
    for back in range(KW):
        part = ext_ref[pl.ds(HALO - back, rows), columns] * taps[KW - 1 - back : KW - back, :]
        if back > 0:
            part = part * live[:, back : back + 1]
        total = part if total is None else total + part
    return total


def head_features(ext_ref, tq, tk, tv, live, rows, width):
    conv = [
        conv_parts(ext_ref, tq, live, pl.ds(0, width), rows),
        conv_parts(ext_ref, tk[:, :width], live, pl.ds(width, width), rows),
        conv_parts(ext_ref, tk[:, width:], live, pl.ds(2 * width, width), rows),
        conv_parts(ext_ref, tv[:, :width], live, pl.ds(3 * width, width), rows),
        conv_parts(ext_ref, tv[:, width:], live, pl.ds(4 * width, width), rows),
    ]
    return conv


def unit_rows(act):
    return lax.rsqrt(jnp.sum(act * act, axis=-1, keepdims=True) + 1e-06)


def greet_group(count):
    place, group = lax.axis_index("seq"), lax.axis_index("dp")
    barrier = pltpu.get_barrier_semaphore()

    def greet(step, carry):
        peer = lax.rem(place + step, count)
        pl.semaphore_signal(barrier, inc=1, device_id=(group, peer), device_id_type=MESH)
        return carry

    lax.fori_loop(1, count, greet, 0)
    return barrier


def carry_steps(count, heads, backward, part_ref, maps_ref, inbox, outbox, landed, sems):
    send_sem, recv_sem, back_sem, land_sem = sems
    place, group = lax.axis_index("seq"), lax.axis_index("dp")
    width = landed.shape[-1]
    stride = count // 16

    def keeper(h):
        return (2 * h + group) * stride

    def outgoing(h):
        return pltpu.make_async_remote_copy(
            src_ref=part_ref.at[h],
            dst_ref=inbox.at[place],
            send_sem=send_sem.at[h],
            recv_sem=recv_sem.at[place],
            device_id=(group, keeper(h)),
            device_id_type=MESH,
        )

    def send(h):
        @pl.when(place != keeper(h))
        def _():
            outgoing(h).start()

        @pl.when(place == keeper(h))
        def _():
            inbox[pl.ds(place, 1)] = part_ref[pl.ds(h, 1)]

    def scan_head(h):
        def returning(where):
            return pltpu.make_async_remote_copy(
                src_ref=outbox.at[where],
                dst_ref=landed.at[h],
                send_sem=back_sem.at[where],
                recv_sem=land_sem.at[h],
                device_id=(group, where),
                device_id_type=MESH,
            )

        def lap(step, state):
            where = count - 1 - step if backward else step
            outbox[pl.ds(where, 1)] = state[None].astype(BF16)

            @pl.when(where != place)
            def _():
                returning(where).start()
                pltpu.make_async_remote_copy(
                    src_ref=part_ref.at[h],
                    dst_ref=inbox.at[where],
                    send_sem=send_sem.at[h],
                    recv_sem=recv_sem.at[where],
                    device_id=(group, where),
                    device_id_type=MESH,
                ).wait_recv()

            @pl.when(where == place)
            def _():
                landed[h : h + 1] = outbox[pl.ds(where, 1)]

            got = inbox[pl.ds(where, 1)][0]
            high, low = halves(state)
            both = jnp.concatenate([high, low], axis=1)
            if backward:
                moved = mm(maps_ref[pl.ds(where, 1)][0][:, width:], both, TN)
            else:
                moved = mm(got[:, width:], both)
            return moved[:, :width] + moved[:, width:] + got[:, :width].astype(F32)

        lax.fori_loop(0, count, lap, jnp.zeros((width, width), F32))

        def finish(where, carry):
            @pl.when(where != place)
            def _():
                returning(where).wait_send()

            return carry

        return lambda: lax.fori_loop(0, count, finish, 0)

    def scan():
        for h in range(heads):

            @pl.when(place == keeper(h))
            def _(h=h):
                scan_head(h)()

    def take():
        for h in range(heads):

            @pl.when(place != keeper(h))
            def _(h=h):
                outgoing(h).wait_send()
                pltpu.make_async_remote_copy(
                    src_ref=outbox.at[0],
                    dst_ref=landed.at[h],
                    send_sem=back_sem.at[0],
                    recv_sem=land_sem.at[h],
                    device_id=(group, keeper(h)),
                    device_id_type=MESH,
                ).wait_recv()

    return send, scan, take


def carry_scratch(count, heads, width, columns):
    dma = pltpu.SemaphoreType.DMA
    return [
        pltpu.VMEM((count, width, columns), BF16),
        pltpu.VMEM((count, width, width), BF16),
        pltpu.VMEM((heads, width, width), BF16),
        dma((heads,)),
        dma((count,)),
        dma((count,)),
        dma((heads,)),
    ]


def mixer_forward_kernel(
    count, every_head, xn_ref, wq_ref, wk_ref, wv_ref, wg_ref, tq_ref, tk_ref, tv_ref, live_ref, acol_ref, arow_ref,
    pre_ref, gate_ref, oloc_ref, oread_ref, inv_ref, delta_ref, state_ref, turn_ref, carry_ref, start_ref, maps_ref,
    ext_ref, part_ref, inbox, outbox, landed, *sems,
):
    heads, rows, width = oread_ref.shape
    turn_at = pl.program_id(0)
    barrier = pltpu.get_barrier_semaphore()

    @pl.when(turn_at == 0)
    def _():
        greet_group(count)

    give, scan, take = carry_steps(count, every_head, False, part_ref, None, inbox, outbox, landed, sems)
    blocks = rows // BLOCK
    xn = xn_ref[...]
    live = live_ref[...]
    gate_ref[...] = mm(xn[HALO:], wg_ref[...])
    query, key, value = mm(xn, wq_ref[...]), mm(xn, wk_ref[...]), mm(xn, wv_ref[...])
    reach, strict, first, merges, eye = step_masks()
    cut = [slice(b * BLOCK, (b + 1) * BLOCK) for b in range(blocks)]
    every = [(n, b) for n in range(heads) for b in range(blocks)]
    qb, kb, vb = {}, {}, {}
    for n in range(heads):
        one, two = slice(n * width, (n + 1) * width), slice(2 * n * width, 2 * (n + 1) * width)
        pre = jnp.concatenate([query[:, one], key[:, two], value[:, two]], axis=1).astype(BF16)
        pre_ref[n] = pre
        ext_ref[n] = pre.astype(F32)
        conv = head_features(ext_ref.at[n], tq_ref[:, one], tk_ref[:, two], tv_ref[:, two], live, rows, width)
        act = [c * sigmoid(c) for c in conv]
        q = (act[0] * unit_rows(act[0]) * width ** (-0.5)).astype(BF16)
        k = [(a * unit_rows(a)).astype(BF16) for a in act[1:3]]
        v = [a.astype(BF16) for a in act[3:5]]
        for b in range(blocks):
            qb[n, b] = q[cut[b]]
            kb[n, b] = jnp.concatenate([k[0][cut[b]], k[1][cut[b]]], axis=0)
            vb[n, b] = jnp.concatenate([v[0][cut[b]], v[1][cut[b]]], axis=0)
    ccol = {at: acol_ref[at[0], at[1], :, 0:1] for at in every}
    bcol = {at: acol_ref[at[0], at[1], :, 1:2] for at in every}
    crow = {at: arow_ref[at[0], at[1], 0:1, :] for at in every}
    brow = {at: arow_ref[at[0], at[1], 1:2, :] for at in every}
    fade = {at: jnp.exp(jnp.where(reach, ccol[at] - crow[at], -1e30)) for at in every}
    system = [jnp.where(strict, fade[at] * mm(kb[at], kb[at], NT), 0.0) * bcol[at] for at in every]
    inv = dict(zip(every, unit_lower_inverse(system, first, merges, eye)))
    for at in every:
        inv_ref[at[0], at[1]] = inv[at].astype(BF16)
    local = {at: mm2(inv[at] * brow[at], vb[at]) for at in every}
    reads = {at: mm2(inv[at] * (brow[at] * jnp.exp(crow[at])), kb[at]) for at in every}
    score = {at: fade[at][:BLOCK] * mm(qb[at], kb[at], NT) for at in every}
    grow = {at: jnp.exp(ccol[at]) for at in every}
    last = {at: ccol[at][BLOCK - 1 : BLOCK] for at in every}
    tail = {at: kb[at].astype(F32) * jnp.exp(last[at] - ccol[at]) for at in every}
    both = {at: jnp.concatenate([local[at], -reads[at]], axis=1).astype(BF16) for at in every}
    turn = {at: mm(tail[at], both[at], TN) for at in every}
    query_out = {at: mm(score[at], both[at]) for at in every}
    state = {}
    for n in range(heads):
        now = jnp.concatenate([jnp.zeros((width, width), F32), eye], axis=1)
        for b in range(blocks):
            at = (n, b)
            state[at] = now
            step = turn[at][:, width:].astype(BF16)
            turn_ref[n, b] = step
            fixed = jnp.concatenate([turn[at][:, :width], jnp.zeros((width, width), F32)], axis=1)
            now = jnp.exp(last[at]) * now + fixed + mm(step, now)
        part_ref[pl.ds(turn_at * heads + n, 1)] = now.astype(BF16)[None]

    @pl.when(turn_at == 0)
    def _():
        pl.semaphore_wait(barrier, count - 1)

    for n in range(heads):
        give(turn_at * heads + n)
    for at in every:
        n, b = at
        carried = query_out[at][:, width:] + grow[at][:BLOCK] * qb[at].astype(F32)
        low = state[at].astype(BF16)
        carry_ref[n, b] = carried.astype(BF16)
        state_ref[n, b] = low
        fixed = jnp.concatenate([local[at], jnp.zeros((STEPS, width), F32)], axis=1)
        delta_ref[n, b] = (fixed - mm(reads[at], low)).astype(BF16)
        out = mm(carried, low)
        oloc_ref[cut[b], n * width : (n + 1) * width] = out[:, :width] + query_out[at][:, :width]
        oread_ref[n, cut[b], :] = out[:, width:].astype(BF16)

    @pl.when(turn_at == pl.num_programs(0) - 1)
    def _():
        scan()
        take()
        start_ref[...] = landed[...]
        maps_ref[...] = inbox[...]


def head_columns(rows, width):
    return pl.BlockSpec((rows, width), lambda h: (0, h))


def whole(shape):
    return pl.BlockSpec(shape, lambda h: (0,) * len(shape))


def per_head(shape, group=1):
    return pl.BlockSpec((group,) + shape, lambda h: (h,) + (0,) * len(shape))


def mixer_forward(xn, w_query, w_key, w_value, w_outgate, taps, live, acol, arow, heads, width, count):
    ext_rows, depth = xn.shape
    rows = ext_rows - HALO
    blocks = rows // BLOCK
    conv_query, conv_key, conv_value = taps
    out = jax.ShapeDtypeStruct
    return pl.pallas_call(
        partial(mixer_forward_kernel, count, heads),
        grid=(heads // FORWARD_HEADS,),
        in_specs=[
            whole((ext_rows, depth)),
            head_columns(depth, FORWARD_HEADS * width),
            head_columns(depth, 2 * FORWARD_HEADS * width),
            head_columns(depth, 2 * FORWARD_HEADS * width),
            head_columns(depth, FORWARD_HEADS * width),
            head_columns(KW, FORWARD_HEADS * width),
            head_columns(KW, 2 * FORWARD_HEADS * width),
            head_columns(KW, 2 * FORWARD_HEADS * width),
            whole(live.shape),
            per_head(acol.shape[1:], FORWARD_HEADS),
            per_head(arow.shape[1:], FORWARD_HEADS),
        ],
        out_specs=[
            per_head((ext_rows, 5 * width), FORWARD_HEADS),
            head_columns(rows, FORWARD_HEADS * width),
            head_columns(rows, FORWARD_HEADS * width),
            per_head((rows, width), FORWARD_HEADS),
            per_head((blocks, STEPS, STEPS), FORWARD_HEADS),
            per_head((blocks, STEPS, 2 * width), FORWARD_HEADS),
            per_head((blocks, width, 2 * width), FORWARD_HEADS),
            per_head((blocks, width, width), FORWARD_HEADS),
            per_head((blocks, BLOCK, width), FORWARD_HEADS),
            whole((heads, width, width)),
            whole((count, width, 2 * width)),
        ],
        out_shape=[
            out((heads, ext_rows, 5 * width), BF16),
            out((rows, heads * width), F32),
            out((rows, heads * width), F32),
            out((heads, rows, width), BF16),
            out((heads, blocks, STEPS, STEPS), BF16),
            out((heads, blocks, STEPS, 2 * width), BF16),
            out((heads, blocks, width, 2 * width), BF16),
            out((heads, blocks, width, width), BF16),
            out((heads, blocks, BLOCK, width), BF16),
            out((heads, width, width), BF16),
            out((count, width, 2 * width), BF16),
        ],
        scratch_shapes=[
            pltpu.VMEM((FORWARD_HEADS, ext_rows, 5 * width), F32),
            pltpu.VMEM((heads, width, 2 * width), BF16),
        ]
        + carry_scratch(count, heads, width, 2 * width),
        compiler_params=pltpu.CompilerParams(
            collective_id=0, has_side_effects=True, vmem_limit_bytes=VMEM_LIMIT
        ),
        cost_estimate=cost(40),
        name="mixer_forward",
    )(xn, w_query, w_key, w_value, w_outgate, conv_query, conv_key, conv_value, live, acol, arow)


def conv_pull(ext_ref, pad_ref, d_conv, taps, live, columns, rows, dtap_ref):
    total = None
    for back in range(KW):
        part = d_conv if back == 0 else d_conv * live[:, back : back + 1]
        source = ext_ref[pl.ds(HALO - back, rows), columns]
        dtap_ref[KW - 1 - back : KW - back, :] = jnp.sum(part * source, axis=0, keepdims=True)
        pad_ref[pl.ds(HALO, rows), :] = part
        moved = pad_ref[pl.ds(back, rows + HALO), :] * taps[KW - 1 - back : KW - back, :]
        total = moved if total is None else total + moved
    return total


def silu_pull(c, grad):
    s = sigmoid(c)
    return grad * (s + c * s * (1.0 - s))


def unit_pull(act, grad, scale):
    r = unit_rows(act)
    return scale * r * (grad - act * (r * r * jnp.sum(act * grad, axis=-1, keepdims=True)))


def mixer_backward_kernel(
    pre_ref, tq_ref, tk_ref, tv_ref, live_ref, acol_ref, arow_ref,
    inv_ref, delta_ref, state_ref, turn_ref, carry_ref, start_ref, after_ref, dout_ref,
    d_ref, dtq_ref, dtk_ref, dtv_ref, aux_ref,
    ext_ref, pad_ref,
):
    heads = pre_ref.shape[0]
    rows = dout_ref.shape[0]
    width = start_ref.shape[-1]
    blocks = rows // BLOCK
    live = live_ref[...]
    every = [(n, b) for n in range(heads) for b in range(blocks)]
    cut = [slice(b * BLOCK, (b + 1) * BLOCK) for b in range(blocks)]
    conv, act, qb, kb, dout = {}, {}, {}, {}, {}
    for n in range(heads):
        one, two = slice(n * width, (n + 1) * width), slice(2 * n * width, 2 * (n + 1) * width)
        ext_ref[n] = pre_ref[n].astype(F32)
        conv[n] = head_features(ext_ref.at[n], tq_ref[:, one], tk_ref[:, two], tv_ref[:, two], live, rows, width)
        act[n] = [c * sigmoid(c) for c in conv[n][:3]]
        q = (act[n][0] * unit_rows(act[n][0]) * width ** (-0.5)).astype(BF16)
        k = [(a * unit_rows(a)).astype(BF16) for a in act[n][1:]]
        for b in range(blocks):
            qb[n, b] = q[cut[b]]
            kb[n, b] = jnp.concatenate([k[0][cut[b]], k[1][cut[b]]], axis=0)
            dout[n, b] = dout_ref[cut[b], one]
    reach, strict, _, _, _ = step_masks()
    ccol = {at: acol_ref[at[0], at[1], :, 0:1] for at in every}
    bcol = {at: acol_ref[at[0], at[1], :, 1:2] for at in every}
    crow = {at: arow_ref[at[0], at[1], 0:1, :] for at in every}
    last = {at: ccol[at][BLOCK - 1 : BLOCK] for at in every}
    grow = {at: jnp.exp(ccol[at]) for at in every}
    weight = {at: jnp.exp(last[at] - ccol[at]) for at in every}
    ahead = {at: mm(carry_ref[at[0], at[1]], dout[at], TN) for at in every}
    after = {}
    for n in range(heads):
        now = after_ref[n].astype(F32)
        for b in range(blocks - 1, -1, -1):
            after[n, b] = now
            now = jnp.exp(last[n, b]) * now + ahead[n, b] + mm(turn_ref[n, b], now, TN)
    fade = {at: jnp.exp(jnp.where(reach, ccol[at] - crow[at], -1e30)) for at in every}
    delta = {
        at: delta_ref[at[0], at[1], :, :width].astype(F32) + mm(delta_ref[at[0], at[1], :, width:], start_ref[at[0]])
        for at in every
    }
    state = {
        at: state_ref[at[0], at[1], :, :width].astype(F32) + mm(state_ref[at[0], at[1], :, width:], start_ref[at[0]])
        for at in every
    }
    score = {at: fade[at][:BLOCK] * mm(qb[at], kb[at], NT) for at in every}
    d_delta = {at: mm(score[at], dout[at], TN) + weight[at] * mm2t(kb[at], after[at]) for at in every}
    d_rhs = {at: mm2t(inv_ref[at[0], at[1]], d_delta[at], TN) for at in every}
    d_score = {at: (fade[at][:BLOCK] * mm(dout[at], delta[at], NT)).astype(BF16) for at in every}
    d_tail = {at: weight[at] * mm(delta[at], after[at], NT) for at in every}
    d_gram = {
        at: jnp.where(strict, -bcol[at] * fade[at] * mm(d_rhs[at], delta[at], NT), 0.0).astype(BF16) for at in every
    }
    dq = {at: mm(grow[at][:BLOCK] * dout[at], state[at], NT) + mm(d_score[at], kb[at]) for at in every}
    dk_row = {
        at: mm(-(bcol[at] * grow[at]) * d_rhs[at], state[at], NT) + mm(d_gram[at], kb[at]) for at in every
    }
    dk_col = {at: mm(d_gram[at], kb[at], TN) + mm(d_score[at], qb[at], TN) + d_tail[at] for at in every}
    tok = lax.broadcasted_iota(jnp.int32, (BLOCK, 1), 0)
    for at in every:
        kf = kb[at].astype(F32)
        d_beta = (1.0 - bcol[at]) * jnp.sum(d_rhs[at] * delta[at], axis=-1, keepdims=True)
        d_log = jnp.sum(kf * (dk_row[at] - dk_col[at]), axis=-1, keepdims=True)
        d_logq = jnp.sum(qb[at].astype(F32) * dq[at], axis=-1, keepdims=True)
        d_last = jnp.sum(kf * d_tail[at]) + jnp.sum(jnp.exp(last[at]) * after[at] * state[at])
        d_token = d_log[:BLOCK] + d_log[BLOCK:] + d_logq + jnp.where(tok == BLOCK - 1, d_last, 0.0)
        aux_ref[at[0], at[1], :, 0:1] = d_beta
        aux_ref[at[0], at[1], 0:BLOCK, 1:2] = d_token
    pad_ref[0:HALO, :] = jnp.zeros((HALO, width), F32)
    pad_ref[pl.ds(HALO + rows, HALO), :] = jnp.zeros((HALO, width), F32)
    for n in range(heads):
        keys = {b: dk_row[n, b] + dk_col[n, b] for b in range(blocks)}
        values = {b: bcol[n, b] * d_rhs[n, b] for b in range(blocks)}
        d_act = [
            jnp.concatenate([dq[n, b] for b in range(blocks)], axis=0),
            jnp.concatenate([keys[b][:BLOCK] for b in range(blocks)], axis=0),
            jnp.concatenate([keys[b][BLOCK:] for b in range(blocks)], axis=0),
            jnp.concatenate([values[b][:BLOCK] for b in range(blocks)], axis=0),
            jnp.concatenate([values[b][BLOCK:] for b in range(blocks)], axis=0),
        ]
        for i, scale in enumerate((width ** (-0.5), 1.0, 1.0)):
            d_act[i] = unit_pull(act[n][i], d_act[i], scale)
        sides = (
            (tq_ref, dtq_ref, n),
            (tk_ref, dtk_ref, 2 * n),
            (tk_ref, dtk_ref, 2 * n + 1),
            (tv_ref, dtv_ref, 2 * n),
            (tv_ref, dtv_ref, 2 * n + 1),
        )
        for i, (tap_ref, dtap_ref, at) in enumerate(sides):
            lanes = pl.ds(at * width, width)
            grad = conv_pull(
                ext_ref.at[n], pad_ref, silu_pull(conv[n][i], d_act[i]), tap_ref[:, lanes], live,
                pl.ds(i * width, width), rows, dtap_ref.at[:, lanes],
            )
            target = pl.ds((5 * n + i) * width, width)
            d_ref[0:rows, target] = grad[HALO:].astype(BF16)
            d_ref[rows : rows + HALO, target] = grad[:HALO].astype(BF16)


def mixer_backward(pre, taps, live, acol, arow, saved, start, after, dout):
    heads, ext_rows, _ = pre.shape
    rows = ext_rows - HALO
    width = start.shape[-1]
    conv_query, conv_key, conv_value = taps
    out = jax.ShapeDtypeStruct
    columns = heads * width
    group = BACKWARD_HEADS
    tap_specs = [head_columns(KW, times * group * width) for times in (1, 2, 2)]
    return pl.pallas_call(
        mixer_backward_kernel,
        grid=(heads // group,),
        in_specs=[per_head(pre.shape[1:], group)]
        + tap_specs
        + [whole(live.shape)]
        + [per_head(value.shape[1:], group) for value in (acol, arow, *saved, start, after)]
        + [head_columns(rows, group * width)],
        out_specs=[head_columns(ext_rows, 5 * group * width)] + tap_specs + [per_head(acol.shape[1:], group)],
        out_shape=[
            out((ext_rows, 5 * columns), BF16),
            out((KW, columns), F32),
            out((KW, 2 * columns), F32),
            out((KW, 2 * columns), F32),
            out(acol.shape, F32),
        ],
        scratch_shapes=[
            pltpu.VMEM((group, ext_rows, 5 * width), F32),
            pltpu.VMEM((rows + 2 * HALO, width), F32),
        ],
        compiler_params=pltpu.CompilerParams(vmem_limit_bytes=VMEM_LIMIT),
        cost_estimate=cost(35),
        name="mixer_backward",
    )(pre, conv_query, conv_key, conv_value, live, acol, arow, *saved, start, after, dout)


def carry_kernel(count, heads, part_ref, maps_ref, result_ref, inbox, outbox, landed, *sems):
    barrier = greet_group(count)
    pl.semaphore_wait(barrier, count - 1)
    send, scan, take = carry_steps(count, heads, True, part_ref, maps_ref, inbox, outbox, landed, sems)
    for h in range(heads):
        send(h)
    scan()
    take()
    result_ref[...] = landed[...]


def carry_back(part, maps, count):
    heads, width, _ = part.shape
    vmem = pl.BlockSpec(memory_space=pltpu.VMEM)
    return pl.pallas_call(
        partial(carry_kernel, count, heads),
        in_specs=[vmem] * 2,
        out_specs=vmem,
        out_shape=jax.ShapeDtypeStruct((heads, width, width), BF16),
        scratch_shapes=carry_scratch(count, heads, width, width),
        compiler_params=pltpu.CompilerParams(
            collective_id=1, has_side_effects=True, vmem_limit_bytes=VMEM_LIMIT
        ),
        cost_estimate=cost(24),
        name="carry_back",
    )(part, maps)


JOBS = 7
JOB = 512
GROUPS = 3
LATE_JOBS = 10
EARLY_LINKS = ((0, 1, 2, 3), (1, 2, 0, 3), (2, 0, 1, 3))
LATE_LINKS = ((0, 1, 2, 3), (1, 0, 2, 3))


def half_rows(lhs, links, sending, lanes=slice(None)):
    edge = lhs.shape[0] // 8
    parts = []
    for second in range(2):
        for third in range(2):
            move = {links[0]: int(sending), links[1]: second, links[2]: third}
            block = 4 * move[0] + 2 * move[1] + move[2]
            parts.append(lhs[block * edge : (block + 1) * edge, lanes])
    return jnp.concatenate(parts, axis=0)


def column_pieces(sizes, begin, end):
    at, pieces = 0, []
    for index, size in enumerate(sizes):
        low, high = max(at, begin), min(at + size, end)
        if low < high:
            pieces.append((index, low - at, low - begin, high - low))
        at += size
    return pieces


def input_pull_kernel(
    d_ref, dg_ref, wq_ref, wk_ref, wv_ref, wg_ref, aux_ref, raw_ref, live_ref, rate_ref, wr_ref, ext_ref,
    x_ref, halo_ref, gain_ref, resid_ref,
    grad_ref, edge_ref, rim_ref, dgain_ref, drates_ref, misc_ref, total_ref, rates_ref,
):
    head = pl.program_id(0)
    rows = dg_ref.shape[0]
    width = dg_ref.shape[1] // PULL_HEADS
    group = PULL_HEADS
    part = None
    for n in range(group):
        d = d_ref[:, n * 5 * width : (n + 1) * 5 * width]
        two = slice(2 * n * width, 2 * (n + 1) * width)
        term = (
            mm(d[:, :width], wq_ref[:, n * width : (n + 1) * width], NT)
            + mm(d[:, width : 3 * width], wk_ref[:, two], NT)
            + mm(d[:, 3 * width :], wv_ref[:, two], NT)
        )
        part = term if part is None else part + term
    more = mm(dg_ref[...], wg_ref[...], NT)

    @pl.when(head == 0)
    def _():
        heads, blocks = aux_ref.shape[:2]
        wide = heads * REFLECTS
        rates_ref[...] = jnp.zeros_like(rates_ref)
        for h in range(heads):
            for b in range(blocks):
                tokens = slice(b * BLOCK, (b + 1) * BLOCK)
                for j in range(REFLECTS):
                    at = h * REFLECTS + j
                    rates_ref[tokens, at : at + 1] = aux_ref[h, b, j * BLOCK : (j + 1) * BLOCK, 0:1]
                rates_ref[tokens, wide + h : wide + h + 1] = aux_ref[h, b, 0:BLOCK, 1:2]
        value, raw = rates_ref[...], raw_ref[...]
        d_log = exact_sum(block_sums(rows, True), value) * live_ref[:, 1:2]
        lane = lax.broadcasted_iota(jnp.int32, raw.shape, 1)
        d_raw = jnp.where(lane < wide, value, -rate_ref[...] * sigmoid(raw) * d_log)
        summed = jnp.where(lane < wide, value, -softplus(raw) * d_log)
        misc_ref[...] = jnp.sum(summed, axis=0, keepdims=True)
        d_raw = d_raw.astype(BF16)
        drates_ref[...] = mm(d_raw, ext_ref[pl.ds(HALO, rows), :], TN)[: drates_ref.shape[0]]
        total_ref[...] = part
        total_ref[0:rows, :] += more + mm(d_raw, wr_ref[...])

    @pl.when(head > 0)
    def _():
        total_ref[...] += part
        total_ref[0:rows, :] += more

    @pl.when(head == pl.num_programs(0) - 1)
    def _():
        grad = total_ref[...]
        unit, pulled = norm_pull(x_ref[...].astype(F32), gain_ref[...], grad[:rows])
        grad_ref[...] = (resid_ref[...] + pulled).astype(BF16)
        halo_unit, _ = norm_pull(halo_ref[...].astype(F32), gain_ref[...], grad[rows:])
        dgain_ref[...] = jnp.sum(grad[:rows] * unit, axis=0, keepdims=True) + jnp.sum(
            grad[rows:] * halo_unit, axis=0, keepdims=True
        )
        edge_ref[0] = grad[rows - HALO : rows]
        edge_ref[1] = x_ref[rows - HALO :, :].astype(F32)
        edge_ref[2] = resid_ref[rows - HALO :, :]
        rim_ref[...] = grad[rows:]


def norm_pull(x, gain, grad):
    r = lax.rsqrt(jnp.mean(x * x, axis=-1, keepdims=True) + 1e-06)
    unit = x * r
    through = grad * gain
    return unit, r * (through - unit * jnp.mean(unit * through, axis=-1, keepdims=True))


PULL_HEADS = 2


def input_pull(d_all, d_outgate, weights, aux, raw, live, rate, w_rates, ext_b, x, halo, gain, d_resid, heads):
    rows, depth = x.shape
    ext_rows = rows + HALO
    width = d_outgate.shape[1] // heads * PULL_HEADS
    out = jax.ShapeDtypeStruct
    w_query, w_key, w_value, w_outgate = weights
    rates = heads * (REFLECTS + 1)
    return pl.pallas_call(
        input_pull_kernel,
        grid=(heads // PULL_HEADS,),
        in_specs=[
            head_columns(ext_rows, 5 * width),
            head_columns(rows, width),
            head_columns(depth, width),
            head_columns(depth, 2 * width),
            head_columns(depth, 2 * width),
            head_columns(depth, width),
            whole(aux.shape),
            whole(raw.shape),
            whole(live.shape),
            whole(rate.shape),
            whole(w_rates.shape),
            whole(ext_b.shape),
            whole(x.shape),
            whole(halo.shape),
            whole((1, depth)),
            whole(d_resid.shape),
        ],
        out_specs=[
            whole((rows, depth)), whole((3, HALO, depth)), whole((HALO, depth)), whole((1, depth)),
            whole((rates, depth)), whole((1, raw.shape[1])),
        ],
        out_shape=[
            out((rows, depth), BF16),
            out((3, HALO, depth), F32),
            out((HALO, depth), F32),
            out((1, depth), F32),
            out((rates, depth), F32),
            out((1, raw.shape[1]), F32),
        ],
        scratch_shapes=[pltpu.VMEM((ext_rows, depth), F32), pltpu.VMEM(raw.shape, F32)],
        compiler_params=pltpu.CompilerParams(vmem_limit_bytes=VMEM_LIMIT),
        cost_estimate=cost(12),
        name="input_pull",
    )(
        d_all, d_outgate, w_query, w_key, w_value, w_outgate, aux, raw, live, rate, w_rates, ext_b,
        x, halo, gain[None, :], d_resid,
    )


def exact_sum(ones, value):
    total = None
    for _ in range(3):
        part = value.astype(BF16)
        value = value - part.astype(F32)
        term = mm(ones, part)
        total = term if total is None else total + term
    return total


def block_sums(rows, reverse):
    shape = (rows, rows)
    one, two = lax.broadcasted_iota(jnp.int32, shape, 0), lax.broadcasted_iota(jnp.int32, shape, 1)
    order = (one <= two) if reverse else (one >= two)
    return ((one // BLOCK == two // BLOCK) & order).astype(BF16)


def softplus(v):
    return jnp.maximum(v, 0.0) + jnp.log1p(jnp.exp(-jnp.abs(v)))


def rates_kernel(
    heads, lengths_ref, x_ref, gain_ref, wbeta_ref, wdecay_ref, bias_in_ref, rate_in_ref,
    ext_ref, raw_ref, live_ref, acol_ref, arow_ref, halo_ref, weight_ref, rate_ref,
    edge_ref, got_ref, sems,
):
    rows = x_ref.shape[0]
    blocks = rows // BLOCK
    wide = heads * REFLECTS
    seq, count = lax.axis_index("seq"), lax.axis_size("seq")
    behind, before = lax.rem(seq + 1, count), lax.rem(seq + count - 1, count)
    barrier = pltpu.get_barrier_semaphore()
    for place in (behind, before):
        pl.semaphore_signal(barrier, inc=1, device_id={"seq": place}, device_id_type=MESH)
    edge_ref[...] = x_ref[rows - HALO :, :]
    copy = pltpu.make_async_remote_copy(
        src_ref=edge_ref,
        dst_ref=got_ref,
        send_sem=sems.at[0],
        recv_sem=sems.at[1],
        device_id={"seq": behind},
        device_id_type=MESH,
    )

    def normed(field):
        field = field.astype(F32)
        return (
            field * lax.rsqrt(jnp.mean(field * field, axis=-1, keepdims=True) + 1e-06) * gain_ref[...]
        ).astype(BF16)

    pl.semaphore_wait(barrier, 2)
    copy.start()
    xn = normed(x_ref[...])
    ext_ref[pl.ds(HALO, rows), :] = xn
    blank = jnp.zeros((128 - wide - heads, wbeta_ref.shape[1]), F32)
    weight = jnp.concatenate([wbeta_ref[...].astype(F32), wdecay_ref[...].astype(F32), blank], axis=0).astype(BF16)
    weight_ref[...] = weight
    empty = jnp.zeros((1, 128 - wide - heads), F32)
    bias = jnp.concatenate([bias_in_ref[...], jnp.zeros((1, heads), F32), empty], axis=1)
    rate = jnp.concatenate([jnp.zeros((1, wide), F32), rate_in_ref[...], empty], axis=1)
    rate_ref[...] = rate
    raw = mm(xn, weight, NT)
    raw_ref[...] = raw
    row = lax.axis_index("seq") * rows + lax.broadcasted_iota(jnp.int32, (rows, 1), 0)
    place, end = row, 0
    for i in range(lengths_ref.shape[1]):
        begin, end = end, end + lengths_ref[0, i] + (SHORTEST - 1)
        place = jnp.where((row >= begin) & (row < end), row - begin, place)
    live_ref[...] = (place >= lax.broadcasted_iota(jnp.int32, (rows, 8), 1)).astype(F32)
    beta = sigmoid(raw + bias)
    log_rate = jnp.where(place == 0, RESET_LOG, -rate * softplus(raw))
    lane = lax.broadcasted_iota(jnp.int32, raw.shape, 1)
    both = jnp.where(lane < wide, beta, exact_sum(block_sums(rows, False), log_rate))
    turned = both.T
    arow_ref[...] = jnp.zeros_like(arow_ref)
    acol_ref[...] = jnp.zeros_like(acol_ref)
    for h in range(heads):
        for b in range(blocks):
            tokens = slice(b * BLOCK, (b + 1) * BLOCK)
            for j in range(REFLECTS):
                steps = slice(j * BLOCK, (j + 1) * BLOCK)
                at = h * REFLECTS + j
                acol_ref[h, b, steps, 0:1] = both[tokens, wide + h : wide + h + 1]
                acol_ref[h, b, steps, 1:2] = both[tokens, at : at + 1]
                arow_ref[h, b, 0:1, steps] = turned[wide + h : wide + h + 1, tokens]
                arow_ref[h, b, 1:2, steps] = turned[at : at + 1, tokens]
    copy.wait()
    halo = jnp.where(seq > 0, got_ref[...].astype(F32), 0.0)
    halo_ref[...] = halo.astype(BF16)
    ext_ref[0:HALO, :] = normed(halo)


def rates_forward(lengths, x, gain, w_beta, w_decay, bias, rate, heads):
    rows, depth = x.shape
    blocks = rows // BLOCK
    out = jax.ShapeDtypeStruct
    vmem = pl.BlockSpec(memory_space=pltpu.VMEM)
    return pl.pallas_call(
        partial(rates_kernel, heads),
        in_specs=[pl.BlockSpec(memory_space=pltpu.SMEM)] + [vmem] * 6,
        out_specs=[vmem] * 8,
        out_shape=[
            out((rows + HALO, depth), BF16),
            out((rows, 128), F32),
            out((rows, 8), F32),
            out((heads, blocks, STEPS, 8), F32),
            out((heads, blocks, 8, STEPS), F32),
            out((HALO, depth), BF16),
            out((128, depth), BF16),
            out((1, 128), F32),
        ],
        scratch_shapes=[
            pltpu.VMEM((HALO, depth), BF16), pltpu.VMEM((HALO, depth), BF16), pltpu.SemaphoreType.DMA((2,)),
        ],
        compiler_params=pltpu.CompilerParams(
            collective_id=4, has_side_effects=True, vmem_limit_bytes=VMEM_LIMIT
        ),
        cost_estimate=cost(6),
        name="rates_forward",
    )(lengths, x, gain[None, :], w_beta.T, w_decay.T, bias[None, :], rate[None, :])


CHUNK = 256
RING = 6


def flip(bit, other):
    return bit + other - 2 * bit * other


def relative_source(depth):
    block = depth // 32
    seq, group = lax.axis_index("seq"), lax.axis_index("dp")
    index = lax.broadcasted_iota(jnp.int32, (depth, 1), 0)
    row, place, side = index % block, (index // block) % 16, index // (16 * block)
    x = flip(seq % 2, place // 8)
    y = flip((seq // 2) % 2, (place // 4) % 2)
    z = flip((seq // 4) % 2, (place // 2) % 2) + 2 * flip(seq // 8, place % 2)
    return ((((group + side) % 2) * 16 + z * 4 + y * 2 + x) * block + row)


def middle_kernel(
    compact, count, oloc_ref, oread_ref, start_ref, gate_ref, ogain_ref, x_ref, ext_ref, mgain_ref, ograd_ref,
    maps_ref, wout_hbm, wgate_hbm, wup_hbm, wdown_hbm,
    block_ref, dout_ref, part_ref, dresid_ref, dmgain_ref, dogain_ref,
    *refs,
):
    if compact:
        products, (own_out, got_out, after_ref) = refs[: 2 * GROUPS], refs[2 * GROUPS : 2 * GROUPS + 3]
        refs = refs[2 * GROUPS + 3 :]
        gated_ref, hidden_ref, dgate_ref, dup_ref, doutgate_ref, mlp_ref, branch_ref = refs[:7]
        gated_got, hidden_got, dgate_got, dup_got, doutgate_got, own_ref, other_ref, got_ref = refs[7:15]
        other_edge, got_edge, core_sem, chunk_sem, inbox, outbox, landed = refs[15:22]
        carry_sems, staged, stage_sem, refs = refs[22:26], refs[26 : 26 + 2 * GROUPS], refs[26 + 2 * GROUPS], refs[27 + 2 * GROUPS :]
    else:
        gated_ref, hidden_ref, dgate_ref, dup_ref, doutgate_ref, mlp_ref, branch_ref = refs[:7]
        refs = refs[7:]
    wout, wgate, wup, wdown, down_ref, dmlp_ref, sem_out, sems = refs
    heads, rows, width = oread_ref.shape
    depth = x_ref.shape[1]
    chunks = hidden_ref.shape[1] // CHUNK
    fetch_out = pltpu.make_async_copy(wout_hbm, wout, sem_out)
    fetch_out.start()

    def lanes_of(c):
        return pl.ds(pl.multiple_of(c * CHUNK, CHUNK), CHUNK)

    def fetches(c):
        slot = c % RING
        return (
            pltpu.make_async_copy(wgate_hbm.at[:, lanes_of(c)], wgate.at[slot], sems.at[slot, 0]),
            pltpu.make_async_copy(wup_hbm.at[:, lanes_of(c)], wup.at[slot], sems.at[slot, 1]),
            pltpu.make_async_copy(wdown_hbm.at[lanes_of(c), :], wdown.at[slot], sems.at[slot, 2]),
        )

    for c in range(RING):
        for copy in fetches(c):
            copy.start()
    core = {"dp": 1 - lax.axis_index("dp")}

    def to_core(source, target, sems, index):
        return pltpu.make_async_remote_copy(
            src_ref=source,
            dst_ref=target,
            send_sem=sems.at[(0,) + index],
            recv_sem=sems.at[(1,) + index],
            device_id=core,
            device_id_type=MESH,
        )

    if compact:
        barrier = greet_group(count)
        pl.semaphore_signal(barrier, inc=1, device_id=core, device_id_type=MESH)
        give, scan, take = carry_steps(
            count, heads, True, part_ref, maps_ref, inbox, outbox, landed, carry_sems
        )
        half = depth // 2
        lane = lax.broadcasted_iota(jnp.int32, (depth, depth), 1)
        chosen = (lane == relative_source(depth)).astype(BF16)
        swaps = []

        def turn(at, value, index):
            turned = mm(chosen, value, NT).astype(BF16)
            cut = slice(at, at + value.shape[0])
            own_ref[:, cut] = turned[:half]
            other_ref[:, cut] = turned[half:]
            swap(other_ref.at[:, cut], got_ref.at[:, cut], index)

        def turn_tokens():
            value = jnp.concatenate([ext_ref[pl.ds(HALO, rows), :], ext_ref[0:HALO, :]], axis=0)
            turned = mm(chosen, value, NT).astype(BF16)
            own_out[...] = turned[:half]
            other_edge[...] = turned[half:]
            swap(other_edge, got_edge, 3)

        def swap(source, target, index):
            swaps.append(to_core(source, target, core_sem, (index,)))
            swaps[-1].start()

    ogain = ogain_ref[...]
    for h in range(heads):
        lanes = slice(h * width, (h + 1) * width)
        out = oloc_ref[:, lanes] + mm(oread_ref[h], start_ref[h])
        dout_ref[:, lanes] = out
        gate = gate_ref[:, lanes]
        r = lax.rsqrt(jnp.mean(out * out, axis=-1, keepdims=True) + 1e-05)
        gated_ref[:, lanes] = (out * r * ogain * (gate * sigmoid(gate))).astype(BF16)
    fetch_out.wait()
    resid = x_ref[...].astype(F32) + mm(gated_ref[...], wout[...])
    dresid_ref[...] = resid
    r = lax.rsqrt(jnp.mean(resid * resid, axis=-1, keepdims=True) + 1e-06)
    mlp_ref[...] = (resid * r * mgain_ref[...]).astype(BF16)
    if compact:
        pl.semaphore_wait(barrier, count)
        swap(gated_ref, gated_got, 4)
    down_ref[...] = jnp.zeros_like(down_ref)
    dmlp_ref[...] = jnp.zeros_like(dmlp_ref)

    def chunk_swaps(c):
        pairs = ((hidden_ref, hidden_got), (dgate_ref, dgate_got), (dup_ref, dup_got))
        return [
            to_core(own.at[:, lanes_of(c)], got.at[:, lanes_of(c)], chunk_sem, (c, i))
            for i, (own, got) in enumerate(pairs)
        ]

    def one(c, carry):
        slot = c % RING
        for copy in fetches(c):
            copy.wait()
        mlp, ograd = mlp_ref[...], ograd_ref[...]
        lanes = lanes_of(c)
        gate, up = mm(mlp, wgate[slot]), mm(mlp, wup[slot])
        d_hidden = mm(ograd, wdown[slot], NT)
        s = sigmoid(gate)
        act = gate * s
        hidden = (act * up).astype(BF16)
        d_gate = (d_hidden * up * (s + act * (1.0 - s))).astype(BF16)
        d_up = (d_hidden * act).astype(BF16)
        hidden_ref[:, lanes] = hidden
        dgate_ref[:, lanes] = d_gate
        dup_ref[:, lanes] = d_up
        if compact:
            for copy in chunk_swaps(c):
                copy.start()
        down_ref[...] += mm(hidden, wdown[slot])
        dmlp_ref[...] += mm(d_gate, wgate[slot], NT) + mm(d_up, wup[slot], NT)

        @pl.when(c + RING < chunks)
        def _():
            for copy in fetches(c + RING):
                copy.start()

        return carry

    lax.fori_loop(0, chunks, one, 0)
    resid = dresid_ref[...]
    block_ref[...] = (resid + down_ref[...]).astype(BF16)
    grad = dmlp_ref[...]
    unit, pulled = norm_pull(resid, mgain_ref[...], grad)
    dmgain_ref[...] = jnp.sum(grad * unit, axis=0, keepdims=True)
    d_resid = ograd_ref[...].astype(F32) + pulled
    dresid_ref[...] = d_resid
    branch_ref[...] = d_resid.astype(BF16)
    dogain = jnp.zeros((1, width), F32)
    for h in range(heads):
        lanes = slice(h * width, (h + 1) * width)
        grad = mm(branch_ref[...], wout[lanes, :], NT)
        out = dout_ref[:, lanes]
        gate = gate_ref[:, lanes]
        r = lax.rsqrt(jnp.mean(out * out, axis=-1, keepdims=True) + 1e-05)
        s = sigmoid(gate)
        unit = out * r
        doutgate_ref[:, lanes] = (grad * unit * ogain * (s + gate * s * (1.0 - s))).astype(BF16)
        through = grad * (gate * s)
        dogain += jnp.sum(through * unit, axis=0, keepdims=True)
        through = through * ogain
        dout = r * (through - unit * jnp.mean(unit * through, axis=-1, keepdims=True))
        dout_ref[:, lanes] = dout
        part_ref[h] = mm(oread_ref[h], dout, TN).astype(BF16)
        if compact:
            give(h)
    dogain_ref[...] = dogain
    if compact:
        turn(0, mlp_ref[...], 0)
        turn(rows, ograd_ref[...], 1)
        swap(doutgate_ref, doutgate_got, 5)
        turn(2 * rows, branch_ref[...], 2)
        turn_tokens()

        def arrived(c, carry):
            for copy in chunk_swaps(c):
                copy.wait()
            return carry

        lax.fori_loop(0, chunks, arrived, 0)
        rhs_own = (dgate_ref, dup_ref, hidden_ref, gated_ref, doutgate_ref)
        rhs_got = (dgate_got, dup_got, hidden_got, gated_got, doutgate_got)
        for copy in swaps[:3]:
            copy.wait()
        lhs_own, lhs_got = (own_ref, own_out), (got_ref, got_edge)
        targets = [staged[2 * group : 2 * group + 2] for group in range(GROUPS)]
        early_products(lhs_own, lhs_got, rhs_own, rhs_got, targets, (0, 1, 2))
        outgoing = [
            pltpu.make_async_copy(source, target, stage_sem.at[i])
            for i, (source, target) in enumerate(zip(staged, products))
        ]
        for copy in outgoing[: 2 * GROUPS - 2]:
            copy.start()
        scan()
        for copy in swaps[3:]:
            copy.wait()
        early_products(lhs_own, lhs_got, rhs_own, rhs_got, targets, (3, 4))
        for copy in outgoing[2 * GROUPS - 2 :]:
            copy.start()
        got_out[...] = got_edge[...]
        for copy in outgoing:
            copy.wait()
        take()
        after_ref[...] = landed[...]


def early_products(lhs_own, lhs_got, rhs_own, rhs_got, targets, which):
    tokens = rhs_own[0].shape[0]
    sizes = [rhs.shape[1] for rhs in rhs_own]
    sides = (0, 0, 1, 2, 3)
    for group in range(GROUPS):
        for sending in (True, False):
            turned = {}
            for job in range(JOBS):
                begin = (group * JOBS + job) * JOB
                for index, column, offset, width in column_pieces(sizes, begin, begin + JOB):
                    if index not in which:
                        continue
                    side = sides[index]
                    if side not in turned:
                        cut = slice(side % 3 * tokens, (side % 3 + 1) * tokens)
                        turned[side] = [
                            half_rows(lhs[side // 3], EARLY_LINKS[group], sending, cut) for lhs in (lhs_own, lhs_got)
                        ]
                    lanes = slice(column, column + width)
                    total = mm(turned[side][0], rhs_own[index][:, lanes]) + mm(
                        turned[side][1], rhs_got[index][:, lanes]
                    )
                    targets[group][0 if sending else 1][job, :, offset : offset + width] = total.astype(BF16)


def middle(
    compact, count, oloc, oread, start, gate_pre, out_gain, x, ext_b, mlp_gain, out_grad, maps,
    w_out, w_gate, w_up, w_down,
):
    heads, rows, width = oread.shape
    depth = x.shape[1]
    ff = w_gate.shape[1]
    out = jax.ShapeDtypeStruct
    vmem, hbm = pl.BlockSpec(memory_space=pltpu.VMEM), pl.BlockSpec(memory_space=pl.ANY)
    columns = heads * width
    chunks = ff // CHUNK
    half = depth // 2
    outs = [
        ((rows, depth), BF16), ((rows, columns), F32), ((heads, width, width), BF16), ((rows, depth), F32),
        ((1, depth), F32), ((1, width), F32),
    ]
    rhs = [((rows, columns), BF16)] + [((rows, ff), BF16)] * 3 + [((rows, columns), BF16)]
    kept = rhs + [((rows, depth), BF16)] * 2
    scratch = []
    dma = pltpu.SemaphoreType.DMA
    if compact:
        product = ((JOBS, half // 2, JOB), BF16)
        outs += [product] * (2 * GROUPS) + [((half, rows + HALO), BF16)] * 2
        outs += [((heads, width, width), BF16), ((rows, columns), BF16)]
        buffers = kept[:4] + kept[5:] + rhs + [((half, 3 * rows), BF16)] * 3 + [((half, rows + HALO), BF16)] * 2
        scratch += [pltpu.VMEM(*buffer) for buffer in buffers] + [dma((2, 6)), dma((2, chunks, 3))]
        scratch += carry_scratch(count, heads, width, width)
        scratch += [pltpu.VMEM(*product)] * (2 * GROUPS) + [dma((2 * GROUPS,))]
    else:
        outs += kept
    scratch += [
        pltpu.VMEM(w_out.shape, BF16),
        pltpu.VMEM((RING, depth, CHUNK), BF16),
        pltpu.VMEM((RING, depth, CHUNK), BF16),
        pltpu.VMEM((RING, CHUNK, depth), BF16),
        pltpu.VMEM((rows, depth), F32),
        pltpu.VMEM((rows, depth), F32),
        dma,
        dma((RING, 3)),
    ]

    def kernel(*refs):
        if not compact:
            middle_kernel(compact, count, *refs)
            return
        late = 20 + 2 * GROUPS + 3
        rest = refs[late + 1 :]
        middle_kernel(compact, count, *refs[:late], *rest[:4], refs[late], *rest[4:])

    params = {"collective_id": 3, "has_side_effects": True} if compact else {}
    return pl.pallas_call(
        kernel,
        in_specs=[vmem] * 10 + [hbm] * 4,
        out_specs=[hbm if compact and shape == product else vmem for shape in outs],
        out_shape=[out(*shape) for shape in outs],
        scratch_shapes=scratch,
        compiler_params=pltpu.CompilerParams(vmem_limit_bytes=VMEM_LIMIT, **params),
        cost_estimate=cost(30),
        name="middle",
    )(
        oloc, oread, start, gate_pre, out_gain[None, :], x, ext_b, mlp_gain[None, :], out_grad, maps,
        w_out, w_gate, w_up, w_down,
    )


def reduce_kernel(
    heads, arr_a, arr_b, arr_c, keep_a, keep_b, keep_c, own_ref, got_ref, rhs_ref, tq_ref, tk_ref, tv_ref, attn_ref, mlp_ref, ogain_ref,
    misc_ref, rates_ref, edge_ref, rim_ref, again_ref,
    gate_out, up_out, down_out, out_out, outgate_out, q_out, k_out, v_out, tq_out, tk_out, tv_out, rest_out,
    edge_out,
    fetched, e_keep, e_send, e_got2, e_got3, e_got4,
    rhs_got, lhs_ref, l_first, l_send, l_keep, l_got1, l_got2, l_got3, l_got4, small_sum, small_got, rim_got,
    dp_sem, e_sem, l_sem, s_sem, f_sem,
):
    seq = lax.axis_index("seq")
    group = lax.axis_index("dp")
    count = lax.axis_size("seq")
    x, y, z = seq % 2, (seq // 2) % 2, seq // 4
    near = (seq + 1 - 2 * x, seq + 2 - 4 * y)
    low_z = seq + 4 - 8 * (z % 2)
    high_z = seq + 8 - 16 * (z // 2)

    def at(place):
        return {"dp": group, "seq": place}

    core = {"dp": 1 - group, "seq": seq}
    before, behind = lax.rem(seq + count - 1, count), lax.rem(seq + 1, count)

    def send(source, target, sems, index, device):
        return pltpu.make_async_remote_copy(
            src_ref=source,
            dst_ref=target,
            send_sem=sems.at[(0,) + index],
            recv_sem=sems.at[(1,) + index],
            device_id=device,
            device_id_type=MESH,
        )

    def fetches(i):
        return [
            pltpu.make_async_copy(source.at[i], fetched.at[j, i], f_sem.at[j, i])
            for j, source in enumerate((arr_a, arr_b, arr_c, keep_a, keep_b, keep_c))
        ]

    def fetch(i, carry):
        for copy in fetches(i):
            copy.start()
        return carry

    lax.fori_loop(0, JOBS, fetch, 0)
    barrier = pltpu.get_barrier_semaphore()
    everyone = [core] + [at(place) for place in (near[0], near[1], low_z, high_z, before, behind)]
    for device in everyone:
        pl.semaphore_signal(barrier, inc=1, device_id=device, device_id_type=MESH)
    rim = send(rim_ref, rim_got, dp_sem, (1,), at(before))
    hops = [core, at(high_z), at(low_z), at(near[0]), at(near[1])]

    def hop(step):
        return send(small_sum.at[step], small_got.at[step], s_sem, (step,), hops[step])

    def next_hop(step):
        hop(step - 1).wait_recv()
        small_sum[step] = small_sum[step - 1] + small_got[step - 1]
        if step < len(hops):
            hop(step).start()

    depth = tq_ref.shape[1]
    small_sum[0, 0:KW] = tq_ref[...]
    for half in range(2):
        lanes = pl.ds(half * depth, depth)
        small_sum[0, KW * (1 + half) : KW * (2 + half)] = tk_ref[:, lanes]
        small_sum[0, KW * (3 + half) : KW * (4 + half)] = tv_ref[:, lanes]
    small_sum[0, 5 * KW : 6 * KW] = jnp.zeros((KW, depth), F32)
    small_sum[0, 5 * KW : 5 * KW + 1] = attn_ref[...]
    small_sum[0, 5 * KW + 1 : 5 * KW + 2] = mlp_ref[...]
    gains = ogain_ref.shape[1]
    small_sum[0, 5 * KW + 2 : 5 * KW + 3, 0:gains] = ogain_ref[...]
    small_sum[0, 5 * KW + 2 : 5 * KW + 3, gains : gains + misc_ref.shape[1]] = misc_ref[...]
    small_sum[0, 6 * KW :] = rates_ref[...]
    for p in range(2):
        for side, lhs in enumerate((own_ref, got_ref)):
            for sending in range(2):
                lhs_ref[p, side, sending] = half_rows(lhs[...], LATE_LINKS[p], sending)
    swap = send(rhs_ref, rhs_got, dp_sem, (0,), core)
    pl.semaphore_wait(barrier, len(everyone))
    hop(0).start()
    swap.start()
    rim.start()

    places = (near[0], near[1], low_z, high_z)
    quarter = e_got2.shape[2]
    eighth, share = quarter // 2, quarter // 4

    def exchange(p, i, stage, sent, got, sems, links):
        begin = (0, 0, quarter, quarter + eighth)[stage]
        target = places[links[p][stage]]
        return send(sent.at[p, i, pl.ds(begin, got.shape[2])], got.at[p, i], sems, (p, i, stage), at(target))

    def early(p, i, stage):
        return exchange(p, i, stage, e_send, (None, e_got2, e_got3, e_got4)[stage], e_sem, EARLY_LINKS)

    def late(p, i, stage):
        sent = l_first if stage == 0 else l_send
        return exchange(p, i, stage, sent, (l_got1, l_got2, l_got3, l_got4)[stage], l_sem, LATE_LINKS)

    def early2(i, carry):
        for copy in fetches(i):
            copy.wait()
        for p in range(GROUPS):
            total = fetched[p, i].astype(F32) + fetched[GROUPS + p, i].astype(F32)
            e_keep[p, i] = total[:quarter].astype(BF16)
            e_send[p, i, 0:quarter] = total[quarter:].astype(BF16)
            early(p, i, 1).start()
        return carry

    def onward(p, i, copy_of, keep, sent, got, stage, begin):
        copy_of(p, i, stage).wait_recv()
        rows = got.shape[2]
        half = rows // 2
        total = keep[p, i, 0:rows].astype(F32) + got[p, i].astype(F32)
        keep[p, i, 0:half] = total[:half].astype(BF16)
        sent[p, i, begin : begin + half] = total[half:].astype(BF16)
        copy_of(p, i, stage + 1).start()

    def later(i, carry, copy_of, keep, sent, got, stage, begin):
        for p in range(keep.shape[0]):
            onward(p, i, copy_of, keep, sent, got, stage, begin)
        return carry

    lax.fori_loop(0, JOBS, early2, 0)
    next_hop(1)
    swap.wait_recv()
    job = l_got1.shape[-1]
    late_jobs = LATE_JOBS // 2
    tokens = rhs_ref.shape[0]

    def product(m, p, sending):
        lanes = pl.ds(pl.multiple_of(m * job, job), job)
        total = mm(lhs_ref[p, 0, int(sending)], rhs_ref[:, lanes]) + mm(
            lhs_ref[p, 1, int(sending)], rhs_got[:, lanes]
        )
        return total[:quarter], total[quarter:]

    def late1(i, carry):
        for p in range(2):
            low, high = product(2 * i + p, p, True)
            l_first[p, i, 0:quarter] = low.astype(BF16)
            l_first[p, i, quarter : 2 * quarter] = high.astype(BF16)
            late(p, i, 0).start()
        return carry

    def late2(i, carry):
        for p in range(2):
            low, high = product(2 * i + p, p, False)
            late(p, i, 0).wait_recv()
            l_keep[p, i] = (low + l_got1[p, i, 0:quarter].astype(F32)).astype(BF16)
            l_send[p, i, 0:quarter] = (high + l_got1[p, i, quarter : 2 * quarter].astype(F32)).astype(BF16)
            late(p, i, 1).start()
        return carry

    lag = JOBS - late_jobs

    def low_turn(i, carry):
        later(i, carry, early, e_keep, e_send, e_got2, 1, quarter)

        @pl.when(i == lag)
        def _():
            next_hop(2)

        @pl.when(i >= lag)
        def _():
            late1(i - lag, carry)

        return carry

    def high_turn(i, carry):
        later(i, carry, early, e_keep, e_send, e_got3, 2, quarter + eighth)

        @pl.when(i >= lag)
        def _():
            late2(i - lag, carry)

        return carry

    lax.fori_loop(0, JOBS, low_turn, 0)
    next_hop(3)
    lax.fori_loop(0, JOBS, high_turn, 0)
    next_hop(4)
    rim.wait_recv()
    inside = (seq < count - 1).astype(F32)
    _, pulled = norm_pull(edge_ref[1], again_ref[...], edge_ref[0] + inside * rim_got[...])
    edge_out[...] = (edge_ref[2] + pulled).astype(BF16)
    late_low = partial(later, copy_of=late, keep=l_keep, sent=l_send, got=l_got2, stage=1, begin=quarter)
    lax.fori_loop(0, late_jobs, late_low, 0)
    next_hop(5)
    late_high = partial(later, copy_of=late, keep=l_keep, sent=l_send, got=l_got3, stage=2, begin=quarter + eighth)
    lax.fori_loop(0, late_jobs, late_high, 0)
    early_outs = (gate_out, up_out, down_out, out_out, outgate_out)
    for i in range(JOBS):
        for p in range(GROUPS):
            early(p, i, 3).wait_recv()
            total = e_keep[p, i, 0:share].astype(F32) + e_got4[p, i].astype(F32)
            first = (p * JOBS + i) * JOB
            for output, to, begin, width in column_pieces([o.shape[1] for o in early_outs], first, first + JOB):
                early_outs[output][:, to : to + width] = total[:, begin : begin + width]
    tq_out[...] = small_sum[5, 0:KW]
    for half in range(2):
        lanes = pl.ds(half * depth, depth)
        tk_out[:, lanes] = small_sum[5, KW * (1 + half) : KW * (2 + half)]
        tv_out[:, lanes] = small_sum[5, KW * (3 + half) : KW * (4 + half)]
    rest_out[...] = small_sum[5, 5 * KW :]
    width = q_out.shape[1] // heads
    for i in range(late_jobs):
        for p in range(2):
            late(p, i, 3).wait_recv()
            total = l_keep[p, i, 0:share].astype(F32) + l_got4[p, i].astype(F32)
            for begin in range(0, job, width):
                head, part = divmod(((2 * i + p) * job + begin) // width, 5)
                if part == 0:
                    target, to = q_out, head * width
                else:
                    target, to = (k_out, v_out)[(part - 1) // 2], (2 * head + (part - 1) % 2) * width
                target[:, to : to + width] = total[:, begin : begin + width]

    def early_sent(i, carry):
        for p in range(GROUPS):
            for stage in (1, 2, 3):
                early(p, i, stage).wait_send()
        return carry

    def late_sent(i, carry):
        for p in range(2):
            for stage in (0, 1, 2, 3):
                late(p, i, stage).wait_send()
        return carry

    lax.fori_loop(0, JOBS, early_sent, 0)
    lax.fori_loop(0, late_jobs, late_sent, 0)
    swap.wait_send()
    rim.wait_send()
    for step in range(len(hops)):
        hop(step).wait_send()


def reduce_all(arrived, kept, own, got, rhs, taps, gains, rates, edge, rim, gain, ff, heads):
    half = own.shape[0] // 2
    quarter, eighth, share = half // 2, half // 4, half // 8
    count = LATE_JOBS // 2
    columns = rhs.shape[1] // 5
    job = rhs.shape[1] // LATE_JOBS
    depth = rates.shape[1]
    small_rows = 6 * KW + rates.shape[0]
    out = jax.ShapeDtypeStruct
    vmem = pl.BlockSpec(memory_space=pltpu.VMEM)

    def stages(groups, jobs, width):
        return [((groups, jobs, rows, width), BF16) for rows in (quarter, eighth, share)]

    buffers = [((2 * GROUPS, JOBS, half, JOB), BF16)]
    buffers += [((GROUPS, JOBS, quarter, JOB), BF16), ((GROUPS, JOBS, half, JOB), BF16)]
    buffers += stages(GROUPS, JOBS, JOB)
    buffers += [(rhs.shape, BF16), ((2, 2, 2, half, own.shape[1]), BF16)] + [((2, count, half, job), BF16)] * 2 + [((2, count, quarter, job), BF16)]
    buffers += [((2, count, half, job), BF16)] + stages(2, count, job)
    buffers += [((6, small_rows, depth), F32), ((5, small_rows, depth), F32), (rim.shape, F32)]
    dma = pltpu.SemaphoreType.DMA
    shapes = [(share, ff)] * 3 + [(share, columns)] * 3 + [(share, 2 * columns)] * 2
    shapes += [tap.shape for tap in taps] + [(small_rows - 5 * KW, depth)]
    return pl.pallas_call(
        partial(reduce_kernel, heads),
        in_specs=[pl.BlockSpec(memory_space=pl.ANY)] * (2 * GROUPS) + [vmem] * 14,
        out_specs=[vmem] * 13,
        out_shape=[out(shape, F32) for shape in shapes] + [out(rim.shape, BF16)],
        scratch_shapes=[pltpu.VMEM(shape, kind) for shape, kind in buffers]
        + [dma((2, 2)), dma((2, GROUPS, JOBS, 4)), dma((2, 2, count, 4)), dma((2, 5)), dma((2 * GROUPS, JOBS))],
        compiler_params=pltpu.CompilerParams(
            collective_id=2, has_side_effects=True, vmem_limit_bytes=VMEM_LIMIT
        ),
        cost_estimate=cost(90),
        name="reduce_all",
    )(*arrived, *kept, own, got, rhs, *taps, *gains, rates, edge, rim, gain)


def finish_kernel(marks, grad_ref, edge_ref, rest_ref, *refs):
    count = (len(refs) - 8) // 2
    sources, (grad_out, *outs) = refs[:count], refs[count:]
    rows = grad_ref.shape[0]
    grad_out[0 : rows - HALO, :] = grad_ref[0 : rows - HALO, :]
    grad_out[rows - HALO :, :] = edge_ref[...]
    for source, target in zip(sources, outs):
        target[...] = source[...]
    again, mlp, beta, rate, gain, bias, decay = outs[count:]
    rest = rest_ref[...]
    share, depth = again.shape[1], rest.shape[1]
    place = lax.axis_index("dp") * lax.axis_size("seq") + lax.axis_index("seq")
    own = pltpu.roll(rest, lax.rem(depth - place * share, depth), 1)[:, :share]
    again[...] = own[0:1]
    mlp[...] = own[1:2]
    beta[...] = own[4 : 4 + beta.shape[0]]
    rate[...] = own[4 + beta.shape[0] :]
    for target, begin in zip((gain, bias, decay), marks):
        target[...] = rest_ref[2:3, begin : begin + target.shape[1]]


def finish(input_grad, edge_grad, rest, values, share, width, heads):
    wide, narrow = heads * REFLECTS, heads
    shapes = [value.shape for value in values]
    shapes += [(1, share)] * 2 + [(wide, share), (narrow, share), (1, width), (1, wide), (1, narrow)]
    out = jax.ShapeDtypeStruct
    vmem = pl.BlockSpec(memory_space=pltpu.VMEM)
    return pl.pallas_call(
        partial(finish_kernel, (0, width, width + wide)),
        in_specs=[vmem] * (3 + len(values)),
        out_specs=[vmem] * (1 + len(shapes)),
        out_shape=[out(input_grad.shape, BF16)] + [out(shape, F32) for shape in shapes],
        compiler_params=pltpu.CompilerParams(vmem_limit_bytes=VMEM_LIMIT),
        cost_estimate=cost(3),
        name="finish",
    )(input_grad, edge_grad, rest, *values)


def dot32(a, b, dims=NN):
    return lax.dot_general(a, b, dims, preferred_element_type=F32)


def swap_core(value):
    count = lax.axis_size("dp")
    return lax.ppermute(value, "dp", [(i, (i + 1) % count) for i in range(count)])


def neighbour_route(bit):
    return [(i, i ^ bit) for i in range(16)]


def by_head(field, heads, begin, size):
    rows = field.shape[0]
    return field.reshape(rows, heads, -1)[:, :, begin : begin + size].reshape(rows, heads * size)


def per_device(
    block_input, lengths, attn_gain, w_query, w_key, w_value, w_outgate, w_beta, w_decay, beta_bias,
    decay_rate, conv_query, conv_key, conv_value, out_gain, w_out, mlp_gain, w_gate, w_up, w_down,
    out_grad,
):
    rows, depth = block_input.shape
    heads = decay_rate.shape[0]
    width = out_gain.shape[0]
    count = lax.axis_size("seq")
    seq = lax.axis_index("seq")
    group = lax.axis_index("dp")
    compact = count == 16
    wide = heads * REFLECTS
    ext_b, raw, live, acol, arow, halo, w_rates, rate = rates_forward(
        lengths, block_input, attn_gain, w_beta, w_decay, beta_bias, decay_rate, heads
    )
    taps = (conv_query, conv_key, conv_value)
    pre, gate_pre, oloc, oread, *saved, start, all_maps = mixer_forward(
        ext_b, w_query, w_key, w_value, w_outgate, taps, live, acol, arow, heads, width, count
    )
    block_output, d_out, part, d_resid, grad_mlp_gain, grad_out_gain, *rest = middle(
        compact, count, oloc, oread, start, gate_pre, out_gain, block_input, ext_b, mlp_gain, out_grad,
        all_maps, w_out, w_gate, w_up, w_down,
    )
    if compact:
        products, (own_l, got_l, after, d_outgate_b) = rest[: 2 * GROUPS], rest[2 * GROUPS :]
        arrived = [
            lax.ppermute(sent, "seq", neighbour_route(1 << links[0])) for sent, links in zip(products[::2], EARLY_LINKS)
        ]
    else:
        gated_b, hidden_b, d_gate_b, d_up_b, d_outgate_b, mlp_b, d_branch_b = rest
        after = carry_back(part, all_maps, count)
    d_all, d_tap_q, d_tap_k, d_tap_v, aux = mixer_backward(
        pre, taps, live, acol, arow, saved, start, after, d_out
    )
    input_grad, edge, rim, grad_attn_gain, grad_rates, misc = input_pull(
        d_all, d_outgate_b, (w_query, w_key, w_value, w_outgate), aux, raw, live, rate, w_rates, ext_b,
        block_input, halo, attn_gain, d_resid, heads,
    )
    last = width + wide + heads
    gains = (grad_attn_gain, grad_mlp_gain, grad_out_gain, misc)
    d_taps = (d_tap_q, d_tap_k, d_tap_v)
    devices = count * lax.axis_size("dp")
    share = depth // devices
    if compact:
        sums = reduce_all(
            arrived, products[1::2], own_l, got_l, d_all, d_taps, gains, grad_rates,
            edge, rim, attn_gain[None, :], w_gate.shape[1], heads,
        )
        trunk, taps_out, rest, edge_grad = sums[5:8], sums[8:11], sums[11], sums[12]
    else:
        normed_e = jnp.concatenate([ext_b[HALO:], ext_b[:HALO]], axis=0)
        normed_b = ext_b[HALO:]
        xf = block_input.astype(F32)
        tail = edge[0] + lax.ppermute(rim, "seq", [(i, i - 1) for i in range(1, count)])
        _, pulled = norm_pull(edge[1], attn_gain[None, :], tail)
        edge_grad = (edge[2] + pulled).astype(BF16)
        line = jnp.pad(jnp.concatenate(gains[2:], axis=1), ((0, 0), (0, depth - width - 128)))
        line = jnp.concatenate([*gains[:2], line, jnp.zeros((1, depth), F32)], axis=0)
        small = lax.psum(d_taps + (line, grad_rates), ("dp", "seq"))
        taps_out, rest = small[:3], jnp.concatenate(small[3:], axis=0)
        trunk = [by_head(d_all, heads, begin * width, size * width) for begin, size in ((0, 1), (1, 2), (3, 2))]
        pairs = zip(
            (mlp_b, mlp_b, out_grad, d_branch_b, normed_b) + (normed_e,) * 3, (d_gate_b, d_up_b, hidden_b, gated_b, d_outgate_b) + tuple(trunk)
        )
        sums = [
            lax.psum_scatter(dot32(lhs, rhs, TN), ("dp", "seq"), scatter_dimension=0, tiled=True)
            for lhs, rhs in pairs
        ]
        trunk = sums[5:]
    values = (*trunk, sums[4], *taps_out, sums[0], sums[1], sums[3], sums[2])
    done = finish(input_grad, edge_grad, rest, values, share, width, heads)
    (
        input_grad, g_query, g_key, g_value, g_outgate, g_conv_q, g_conv_k, g_conv_v, g_gate, g_up, g_out, g_down,
        g_attn, g_mlp, g_beta, g_decay, g_gain, g_bias, g_rate,
    ) = done
    return (
        block_output,
        input_grad,
        g_attn[0],
        g_query,
        g_key,
        g_value,
        g_outgate,
        g_beta.T,
        g_decay.T,
        g_bias[0],
        g_rate[0],
        g_conv_q,
        g_conv_k,
        g_conv_v,
        g_gain[0],
        g_out.T,
        g_mlp[0],
        g_gate,
        g_up,
        g_down.T,
    )


def solution(mesh):
    tokens = P(("dp", "seq"), None)
    column = P(None, ("dp", "seq"))
    vector = P(("dp", "seq"))
    in_specs = (tokens, P("dp", None)) + (P(),) * 18 + (tokens,)
    out_specs = (
        (tokens, tokens, vector)
        + (tokens,) * 6
        + (P(),) * 6
        + (column, vector, tokens, tokens, column)
    )
    return jax.shard_map(
        per_device, mesh=mesh, in_specs=in_specs, out_specs=out_specs, check_vma=False
    )
```

profile of v0, /device:TPU:0, one launch (start us, length us, event | category | flops | bytes accessed | tf_op | source)
XLA Modules:
  0.0 264.0 jit_solution(15365276930987600793)
XLA Ops:
  0.7 12.1 %rates_forward.1 = (bf16[264,1024]{1,0:T(8,128)(2,1)}, f32[256,128]{1,0:T(8,128)}, f32[256,8]{1,0:T(8,128)}, f32[8,4,128,8]{3,2,1,0:T(8,128)}, f32[8,4,8,128]{3,...) custom-call(s32[1,2]{1,0:T(1,128)} %lengths_ref.1, bf16[256,1024]{1,0:T(8,128)(2,1)} %x_ref.3, ...), custom_call_target="tpu_custom_call" | custom-call | flops 6000000000 | bytes 6000000 | tf_op jit(solution)/shard_map/rates_forward/pallas_call | solution.py:854
  12.8 38.2 %mixer_forward.1 = (bf16[8,264,640]{2,1,0:T(8,128)(2,1)}, f32[256,1024]{1,0:T(8,128)}, f32[256,1024]{1,0:T(8,128)}, bf16[8,256,128]{2,1,0:T(8,128)(2,1)}, bf16[8...) custom-call(bf16[264,1024]{1,0:T(8,128)(2,1)} %get-tuple-element.97., ...), custom_call_target="tpu_custom_call" | custom-call | flops 40000000000 | bytes 40000000 | tf_op jit(solution)/shard_map/mixer_forward/pallas_call | solution.py:361
  50.9 62.6 %middle.1 = (bf16[256,1024]{1,0:T(8,128)(2,1)}, f32[256,1024]{1,0:T(8,128)}, bf16[8,128,128]{2,1,0:T(8,128)(2,1)}, f32[256,1024]{1,0:T(8,128)}, f32[1,1024]{1,0:...) custom-call(f32[256,1024]{1,0:T(8,128)} %get-tuple-element.101.refs_, ...), custom_call_target="tpu_custom_call" | custom-call | flops 30000001024 | bytes 30000000 | tf_op jit(solution)/shard_map/middle/pallas_call | solution.py:1173
  113.6 1.2 collective-permute-start
  114.7 0.0 collective-permute-start.1
  114.8 0.0 collective-permute-start.2
  114.8 27.8 %mixer_backward.1 = (bf16[264,5120]{1,0:T(8,128)(2,1)}, f32[4,1024]{1,0:T(4,128)}, f32[4,2048]{1,0:T(4,128)}, f32[4,2048]{1,0:T(4,128)}, f32[8,4,128,8]{3,2,1,0:T(8,128)}) custom-call(bf16[8,264,640]{2,1,0:T(8,128)(2,1)} %get-tuple-element.107.pre_ref, f32[4,1024]{1,0:T(4,128)} %tq_ref.3, f32[4,2048]{1,0:T(4,128)} %tk_ref.3, f32[4,2048]{1,0:T(4,128)} %tv_ref.3, ...), custom_call_target="tpu_custom_call" | custom-call | flops 35000000512 | bytes 35000000 | tf_op jit(solution)/shard_map/mixer_backward/pallas_call | solution.py:550
  142.6 13.3 %input_pull.1 = (bf16[256,1024]{1,0:T(8,128)(2,1)}, f32[3,8,1024]{2,1,0:T(8,128)}, f32[8,1024]{1,0:T(8,128)}, f32[1,1024]{1,0:T(1,128)}, f32[24,1024]{1,0:T(8,128)}, /*index=5*/f32[1,128]{1,0:T(1,128)}) custom-call(bf16[264,5120]{1,0:T(8,128)(2,1)} %get-tuple-element.115.d_ref.rhs_ref, bf16[256,1024]{1,0:T(8,128)(2,1)} %get-tuple-element.116.dg_ref, ...), custom_call_target="tpu_custom_call" | custom-call | flops 12000000000 | bytes 12000000 | tf_op jit(solution)/shard_map/input_pull/pallas_call | solution.py:714
  155.8 0.0 collective-permute-done.arr_a
  155.8 0.0 copy-start.1
  155.9 0.0 collective-permute-done.1.arr_b
  155.9 0.0 copy-start.2
  155.9 0.0 collective-permute-done.2.arr_c
  155.9 0.0 copy-start.3
  155.9 1.2 copy-done.1
  157.1 0.6 copy-done.2
  157.7 0.5 copy-done.3
  158.2 101.6 %reduce_all.1 = (f32[32,2816]{1,0:T(8,128)}, f32[32,2816]{1,0:T(8,128)}, f32[32,2816]{1,0:T(8,128)}, f32[32,1024]{1,0:T(8,128)}, f32[32,1024]{1,0:T(8,128)}, /*i...) custom-call(bf16[7,256,512]{2,1,0:T(8,128)(2,1)} %copy-done.1, ...), custom_call_target="tpu_custom_call" | custom-call | flops 89999998976 | bytes 90000000 | tf_op jit(solution)/shard_map/reduce_all/pallas_call | solution.py:1450
  259.8 0.0 copy-start
  259.9 3.4 %finish.1 = (bf16[256,1024]{1,0:T(8,128)(2,1)}, f32[32,1024]{1,0:T(8,128)}, f32[32,2048]{1,0:T(8,128)}, f32[32,2048]{1,0:T(8,128)}, f32[32,1024]{1,0:T(8,128)}, ...) custom-call(bf16[256,1024]{1,0:T(8,128)(2,1)} %get-tuple-element.123, ...), custom_call_target="tpu_custom_call" | custom-call | flops 3000000000 | bytes 3000000 | tf_op jit(solution)/shard_map/finish/pallas_call | solution.py:1492
  263.2 0.0 copy-done
  263.2 0.8 copy.42
Async XLA Ops:
  113.6 42.3 %collective-permute-start = (bf16[7,256,512]{2,1,0:T(8,128)(2,1)}, bf16[7,256,512]{2,1,0:T(8,128)(2,1)S(1)}, u32[]{:S(2)}, u32[]{:S(2)}) collective-permute-start(bf16[7,256,512]{2,1,0:T(8,128)(2,1)} %get-tuple-element.124), channel_id=1, source_target_pairs={{0,1},{1,0},{2,3},{3,2},{4,5},{5,4},{6,7},{7,6},{8,9},{9,8},{10,11... | collective-permute-start | bytes 5505032 | tf_op jit(solution)/shard_map/ppermute | solution.py:1548
  114.7 41.1 %collective-permute-start.1 = (bf16[7,256,512]{2,1,0:T(8,128)(2,1)}, bf16[7,256,512]{2,1,0:T(8,128)(2,1)S(1)}, u32[]{:S(2)}, u32[]{:S(2)}) collective-permute-start(bf16[7,256,512]{2,1,0:T(8,128)(2,1)} %get-tuple-element.125), channel_id=1, source_target_pairs={{0,2},{1,3},{2,0},{3,1},{4,6},{5,7},{6,4},{7,5},{8,10},{9,11},{10,... | collective-permute-start | bytes 5505032 | tf_op jit(solution)/shard_map/ppermute | solution.py:1548
  114.8 41.1 %collective-permute-start.2 = (bf16[7,256,512]{2,1,0:T(8,128)(2,1)}, bf16[7,256,512]{2,1,0:T(8,128)(2,1)S(1)}, u32[]{:S(2)}, u32[]{:S(2)}) collective-permute-start(bf16[7,256,512]{2,1,0:T(8,128)(2,1)} %get-tuple-element.126), channel_id=1, source_target_pairs={{0,4},{1,5},{2,6},{3,7},{4,0},{5,1},{6,2},{7,3},{8,12},{9,13},{10,... | collective-permute-start | bytes 5505032 | tf_op jit(solution)/shard_map/ppermute | solution.py:1548
  155.8 1.3 copy-start.1
  155.9 1.9 copy-start.2
  155.9 2.3 copy-start.3
  259.8 3.4 %copy-start = (bf16[256,1024]{1,0:T(8,128)(2,1)S(1)}, bf16[256,1024]{1,0:T(8,128)(2,1)}, u32[]{:S(2)}) copy-start(bf16[256,1024]{1,0:T(8,128)(2,1)} %get-tuple-element.194) | copy-start | bytes 1572868
where the time goes:
time: 264 us
  Pallas kernels  259 us (98%)
  local copies, waits for them, and re-layouts  3.12 us (1%)
    pallas_call x1, Pallas kernels, reduce_all(): pl.pallas_call(partial(reduce_kernel, heads), in_specs=[pl.BlockSpec(memo...  102 us
    pallas_call x1, Pallas kernels, middle(): pl.pallas_call(kernel, in_specs=[vmem] * 10 + [hbm] * 4, out_specs=[hbm i...  62.6 us
    pallas_call x1, Pallas kernels, mixer_forward(): pl.pallas_call(partial(mixer_forward_kernel, count, heads), grid=(heads /...  38.2 us
    pallas_call x1, Pallas kernels, mixer_backward(): pl.pallas_call(mixer_backward_kernel, grid=(heads // group,), in_specs=[p...  27.8 us
    pallas_call x1, Pallas kernels, input_pull(): pl.pallas_call(input_pull_kernel, grid=(heads // PULL_HEADS,), in_specs=[...  13.3 us
    pallas_call x1, Pallas kernels, rates_forward(): pl.pallas_call(partial(rates_kernel, heads), in_specs=[pl.BlockSpec(memor...  12.1 us
  transfers between devices with their start and end apart: 3, of which 0 were waited for; matrix products, arithmetic and copies ran while one was open for 0% of the time, Pallas kernels for 16%

commit v1 on v0

--- a/solution.py
+++ b/solution.py
@@ -1191,7 +1191,7 @@
     gate_out, up_out, down_out, out_out, outgate_out, q_out, k_out, v_out, tq_out, tk_out, tv_out, rest_out,
     edge_out,
     fetched, e_keep, e_send, e_got2, e_got3, e_got4,
-    rhs_got, lhs_ref, l_first, l_send, l_keep, l_got1, l_got2, l_got3, l_got4, small_sum, small_got, rim_got,
+    rhs_got, lhs_ref, l_first, l_send, l_keep, l_got1, l_got2, l_got3, l_got4, small_sum, small_send, small_got, rim_got,
     dp_sem, e_sem, l_sem, s_sem, f_sem,
 ):
     seq = lax.axis_index("seq")
@@ -1238,13 +1238,16 @@
     hops = [core, at(high_z), at(low_z), at(near[0]), at(near[1])]
 
     def hop(step):
-        return send(small_sum.at[step], small_got.at[step], s_sem, (step,), hops[step])
+        return send(small_send.at[step], small_got.at[step], s_sem, (step,), hops[step])
 
     def next_hop(step):
         hop(step - 1).wait_recv()
-        small_sum[step] = small_sum[step - 1] + small_got[step - 1]
+        total = small_send[step - 1].astype(F32) + small_got[step - 1].astype(F32)
         if step < len(hops):
+            small_send[step] = total.astype(BF16)
             hop(step).start()
+        else:
+            small_sum[1] = total
 
     depth = tq_ref.shape[1]
     small_sum[0, 0:KW] = tq_ref[...]
@@ -1263,6 +1266,7 @@
         for side, lhs in enumerate((own_ref, got_ref)):
             for sending in range(2):
                 lhs_ref[p, side, sending] = half_rows(lhs[...], LATE_LINKS[p], sending)
+    small_send[0] = small_sum[0].astype(BF16)
     swap = send(rhs_ref, rhs_got, dp_sem, (0,), core)
     pl.semaphore_wait(barrier, len(everyone))
     hop(0).start()
@@ -1385,12 +1389,12 @@
             first = (p * JOBS + i) * JOB
             for output, to, begin, width in column_pieces([o.shape[1] for o in early_outs], first, first + JOB):
                 early_outs[output][:, to : to + width] = total[:, begin : begin + width]
-    tq_out[...] = small_sum[5, 0:KW]
+    tq_out[...] = small_sum[1, 0:KW]
     for half in range(2):
         lanes = pl.ds(half * depth, depth)
-        tk_out[:, lanes] = small_sum[5, KW * (1 + half) : KW * (2 + half)]
-        tv_out[:, lanes] = small_sum[5, KW * (3 + half) : KW * (4 + half)]
-    rest_out[...] = small_sum[5, 5 * KW :]
+        tk_out[:, lanes] = small_sum[1, KW * (1 + half) : KW * (2 + half)]
+        tv_out[:, lanes] = small_sum[1, KW * (3 + half) : KW * (4 + half)]
+    rest_out[...] = small_sum[1, 5 * KW :]
     width = q_out.shape[1] // heads
     for i in range(late_jobs):
         for p in range(2):
@@ -1443,7 +1447,7 @@
     buffers += stages(GROUPS, JOBS, JOB)
     buffers += [(rhs.shape, BF16), ((2, 2, 2, half, own.shape[1]), BF16)] + [((2, count, half, job), BF16)] * 2 + [((2, count, quarter, job), BF16)]
     buffers += [((2, count, half, job), BF16)] + stages(2, count, job)
-    buffers += [((6, small_rows, depth), F32), ((5, small_rows, depth), F32), (rim.shape, F32)]
+    buffers += [((2, small_rows, depth), F32)] + [((5, small_rows, depth), BF16)] * 2 + [(rim.shape, F32)]
     dma = pltpu.SemaphoreType.DMA
     shapes = [(share, ff)] * 3 + [(share, columns)] * 3 + [(share, 2 * columns)] * 2
     shapes += [tap.shape for tap in taps] + [(small_rows - 5 * KW, depth)]
@@ -1485,15 +1489,15 @@
 
 def finish(input_grad, edge_grad, rest, values, share, width, heads):
     wide, narrow = heads * REFLECTS, heads
-    shapes = [value.shape for value in values]
-    shapes += [(1, share)] * 2 + [(wide, share), (narrow, share), (1, width), (1, wide), (1, narrow)]
+    shapes = [(value.shape, value.dtype) for value in values]
+    shapes += [(shape, F32) for shape in [(1, share)] * 2 + [(wide, share), (narrow, share), (1, width), (1, wide), (1, narrow)]]
     out = jax.ShapeDtypeStruct
     vmem = pl.BlockSpec(memory_space=pltpu.VMEM)
     return pl.pallas_call(
         partial(finish_kernel, (0, width, width + wide)),
         in_specs=[vmem] * (3 + len(values)),
         out_specs=[vmem] * (1 + len(shapes)),
-        out_shape=[out(input_grad.shape, BF16)] + [out(shape, F32) for shape in shapes],
+        out_shape=[out(input_grad.shape, BF16)] + [out(*shape) for shape in shapes],
         compiler_params=pltpu.CompilerParams(vmem_limit_bytes=VMEM_LIMIT),
         cost_estimate=cost(3),
         name="finish",
@@ -1588,10 +1592,10 @@
             for lhs, rhs in pairs
         ]
         trunk = sums[5:]
-    values = (*trunk, sums[4], *taps_out, sums[0], sums[1], sums[3], sums[2])
+    values = (block_output, *trunk, sums[4], *taps_out, sums[0], sums[1], sums[3], sums[2])
     done = finish(input_grad, edge_grad, rest, values, share, width, heads)
     (
-        input_grad, g_query, g_key, g_value, g_outgate, g_conv_q, g_conv_k, g_conv_v, g_gate, g_up, g_out, g_down,
+        input_grad, block_output, g_query, g_key, g_value, g_outgate, g_conv_q, g_conv_k, g_conv_v, g_gate, g_up, g_out, g_down,
         g_attn, g_mlp, g_beta, g_decay, g_gain, g_bias, g_rate,
     ) = done
     return (

time: 264 us -> 262 us (level)
  no operation moved by 1% of the time
where the time goes in v1:
time: 262 us
  Pallas kernels  257 us (98%)
    pallas_call x1, Pallas kernels, reduce_all(): pl.pallas_call(partial(reduce_kernel, heads), in_specs=[pl.BlockSpec(memo...  99.5 us
    pallas_call x1, Pallas kernels, middle(): pl.pallas_call(kernel, in_specs=[vmem] * 10 + [hbm] * 4, out_specs=[hbm i...  62.6 us
    pallas_call x1, Pallas kernels, mixer_forward(): pl.pallas_call(partial(mixer_forward_kernel, count, heads), grid=(heads /...  38.1 us
    pallas_call x1, Pallas kernels, mixer_backward(): pl.pallas_call(mixer_backward_kernel, grid=(heads // group,), in_specs=[p...  27.8 us
    pallas_call x1, Pallas kernels, input_pull(): pl.pallas_call(input_pull_kernel, grid=(heads // PULL_HEADS,), in_specs=[...  13.3 us
    pallas_call x1, Pallas kernels, rates_forward(): pl.pallas_call(partial(rates_kernel, heads), in_specs=[pl.BlockSpec(memor...  12.1 us
  transfers between devices with their start and end apart: 3, of which 0 were waited for; matrix products, arithmetic and copies ran while one was open for 0% of the time, Pallas kernels for 16%

profile of v1, /device:TPU:0, one launch (start us, length us, event | category | flops | bytes accessed | tf_op | source)
XLA Modules:
  0.0 261.5 jit_solution(10923753714111452530)
XLA Ops:
  0.7 12.1 %rates_forward.1 = (bf16[264,1024]{1,0:T(8,128)(2,1)}, f32[256,128]{1,0:T(8,128)}, f32[256,8]{1,0:T(8,128)}, f32[8,4,128,8]{3,2,1,0:T(8,128)}, f32[8,4,8,128]{3,...) custom-call(s32[1,2]{1,0:T(1,128)} %lengths_ref.1, bf16[256,1024]{1,0:T(8,128)(2,1)} %x_ref.3, ...), custom_call_target="tpu_custom_call" | custom-call | flops 6000000000 | bytes 6000000 | tf_op jit(solution)/shard_map/rates_forward/pallas_call | solution.py:854
  12.8 38.1 %mixer_forward.1 = (bf16[8,264,640]{2,1,0:T(8,128)(2,1)}, f32[256,1024]{1,0:T(8,128)}, f32[256,1024]{1,0:T(8,128)}, bf16[8,256,128]{2,1,0:T(8,128)(2,1)}, bf16[8...) custom-call(bf16[264,1024]{1,0:T(8,128)(2,1)} %get-tuple-element.98., ...), custom_call_target="tpu_custom_call" | custom-call | flops 40000000000 | bytes 40000000 | tf_op jit(solution)/shard_map/mixer_forward/pallas_call | solution.py:361
  50.9 62.6 %middle.1 = (bf16[256,1024]{1,0:T(8,128)(2,1)}, f32[256,1024]{1,0:T(8,128)}, bf16[8,128,128]{2,1,0:T(8,128)(2,1)}, f32[256,1024]{1,0:T(8,128)}, f32[1,1024]{1,0:...) custom-call(f32[256,1024]{1,0:T(8,128)} %get-tuple-element.109.refs_, ...), custom_call_target="tpu_custom_call" | custom-call | flops 30000001024 | bytes 30000000 | tf_op jit(solution)/shard_map/middle/pallas_call | solution.py:1173
  113.5 1.2 collective-permute-start
  114.7 0.0 collective-permute-start.1
  114.7 0.0 collective-permute-start.2
  114.7 27.8 %mixer_backward.1 = (bf16[264,5120]{1,0:T(8,128)(2,1)}, f32[4,1024]{1,0:T(4,128)}, f32[4,2048]{1,0:T(4,128)}, f32[4,2048]{1,0:T(4,128)}, f32[8,4,128,8]{3,2,1,0:T(8,128)}) custom-call(bf16[8,264,640]{2,1,0:T(8,128)(2,1)} %get-tuple-element.102.pre_ref, f32[4,1024]{1,0:T(4,128)} %tq_ref.3, f32[4,2048]{1,0:T(4,128)} %tk_ref.3, f32[4,2048]{1,0:T(4,128)} %tv_ref.3, ...), custom_call_target="tpu_custom_call" | custom-call | flops 35000000512 | bytes 35000000 | tf_op jit(solution)/shard_map/mixer_backward/pallas_call | solution.py:550
  142.5 13.3 %input_pull.1 = (bf16[256,1024]{1,0:T(8,128)(2,1)}, f32[3,8,1024]{2,1,0:T(8,128)}, f32[8,1024]{1,0:T(8,128)}, f32[1,1024]{1,0:T(1,128)}, f32[24,1024]{1,0:T(8,128)}, /*index=5*/f32[1,128]{1,0:T(1,128)}) custom-call(bf16[264,5120]{1,0:T(8,128)(2,1)} %get-tuple-element.115.d_ref.rhs_ref, bf16[256,1024]{1,0:T(8,128)(2,1)} %get-tuple-element.116.dg_ref, ...), custom_call_target="tpu_custom_call" | custom-call | flops 12000000000 | bytes 12000000 | tf_op jit(solution)/shard_map/input_pull/pallas_call | solution.py:714
  155.8 0.0 collective-permute-done.arr_a
  155.8 0.0 copy-start
  155.8 0.0 collective-permute-done.1.arr_b
  155.8 0.0 copy-start.1
  155.8 0.0 collective-permute-done.2.arr_c
  155.8 0.0 copy-start.2
  155.8 1.2 copy-done
  157.0 0.6 copy-done.1
  157.7 0.5 copy-done.2
  158.1 99.5 %reduce_all.1 = (f32[32,2816]{1,0:T(8,128)}, f32[32,2816]{1,0:T(8,128)}, f32[32,2816]{1,0:T(8,128)}, f32[32,1024]{1,0:T(8,128)}, f32[32,1024]{1,0:T(8,128)}, /*i...) custom-call(bf16[7,256,512]{2,1,0:T(8,128)(2,1)} %copy-done, ...), custom_call_target="tpu_custom_call" | custom-call | flops 89999998976 | bytes 90000000 | tf_op jit(solution)/shard_map/reduce_all/pallas_call | solution.py:1454
  257.7 3.7 %finish.1 = (bf16[256,1024]{1,0:T(8,128)(2,1)}, bf16[256,1024]{1,0:T(8,128)(2,1)}, f32[32,1024]{1,0:T(8,128)}, f32[32,2048]{1,0:T(8,128)}, f32[32,2048]{1,0:T(8,...) custom-call(bf16[256,1024]{1,0:T(8,128)(2,1)} %get-tuple-element.123, ...), custom_call_target="tpu_custom_call" | custom-call | flops 3000000000 | bytes 3000000 | tf_op jit(solution)/shard_map/finish/pallas_call | solution.py:1496
Async XLA Ops:
  113.5 42.3 %collective-permute-start = (bf16[7,256,512]{2,1,0:T(8,128)(2,1)}, bf16[7,256,512]{2,1,0:T(8,128)(2,1)S(1)}, u32[]{:S(2)}, u32[]{:S(2)}) collective-permute-start(bf16[7,256,512]{2,1,0:T(8,128)(2,1)} %get-tuple-element.124), channel_id=1, source_target_pairs={{0,1},{1,0},{2,3},{3,2},{4,5},{5,4},{6,7},{7,6},{8,9},{9,8},{10,11... | collective-permute-start | bytes 5505032 | tf_op jit(solution)/shard_map/ppermute | solution.py:1552
  114.7 41.1 %collective-permute-start.1 = (bf16[7,256,512]{2,1,0:T(8,128)(2,1)}, bf16[7,256,512]{2,1,0:T(8,128)(2,1)S(1)}, u32[]{:S(2)}, u32[]{:S(2)}) collective-permute-start(bf16[7,256,512]{2,1,0:T(8,128)(2,1)} %get-tuple-element.125), channel_id=1, source_target_pairs={{0,2},{1,3},{2,0},{3,1},{4,6},{5,7},{6,4},{7,5},{8,10},{9,11},{10,... | collective-permute-start | bytes 5505032 | tf_op jit(solution)/shard_map/ppermute | solution.py:1552
  114.7 41.1 %collective-permute-start.2 = (bf16[7,256,512]{2,1,0:T(8,128)(2,1)}, bf16[7,256,512]{2,1,0:T(8,128)(2,1)S(1)}, u32[]{:S(2)}, u32[]{:S(2)}) collective-permute-start(bf16[7,256,512]{2,1,0:T(8,128)(2,1)} %get-tuple-element.126), channel_id=1, source_target_pairs={{0,4},{1,5},{2,6},{3,7},{4,0},{5,1},{6,2},{7,3},{8,12},{9,13},{10,... | collective-permute-start | bytes 5505032 | tf_op jit(solution)/shard_map/ppermute | solution.py:1552
  155.8 1.2 copy-start
  155.8 1.9 copy-start.1
  155.8 2.3 copy-start.2

commit v2 on v1

--- a/solution.py
+++ b/solution.py
@@ -1353,9 +1353,9 @@
         def _():
             next_hop(2)
 
-        @pl.when(i >= lag)
+        @pl.when(i < late_jobs)
         def _():
-            late1(i - lag, carry)
+            late1(i, carry)
 
         return carry
 

time: 262 us -> 262 us (level)
  no operation moved by 1% of the time
where the time goes in v2:
time: 262 us; the launch traced here: 261 us
  Pallas kernels  257 us (98%)
    pallas_call x1, Pallas kernels, reduce_all(): pl.pallas_call(partial(reduce_kernel, heads), in_specs=[pl.BlockSpec(memo...  99.5 us
    pallas_call x1, Pallas kernels, middle(): pl.pallas_call(kernel, in_specs=[vmem] * 10 + [hbm] * 4, out_specs=[hbm i...  62.6 us
    pallas_call x1, Pallas kernels, mixer_forward(): pl.pallas_call(partial(mixer_forward_kernel, count, heads), grid=(heads /...  38.1 us
    pallas_call x1, Pallas kernels, mixer_backward(): pl.pallas_call(mixer_backward_kernel, grid=(heads // group,), in_specs=[p...  27.8 us
    pallas_call x1, Pallas kernels, input_pull(): pl.pallas_call(input_pull_kernel, grid=(heads // PULL_HEADS,), in_specs=[...  13.3 us
    pallas_call x1, Pallas kernels, rates_forward(): pl.pallas_call(partial(rates_kernel, heads), in_specs=[pl.BlockSpec(memor...  12.1 us
  transfers between devices with their start and end apart: 3, of which 0 were waited for; matrix products, arithmetic and copies ran while one was open for 0% of the time, Pallas kernels for 16%

profile of v2, /device:TPU:0, one launch (start us, length us, event | category | flops | bytes accessed | tf_op | source)
XLA Modules:
  0.0 261.5 jit_solution(12187340623821770107)
XLA Ops:
  0.7 12.1 %rates_forward.1 = (bf16[264,1024]{1,0:T(8,128)(2,1)}, f32[256,128]{1,0:T(8,128)}, f32[256,8]{1,0:T(8,128)}, f32[8,4,128,8]{3,2,1,0:T(8,128)}, f32[8,4,8,128]{3,...) custom-call(s32[1,2]{1,0:T(1,128)} %lengths_ref.1, bf16[256,1024]{1,0:T(8,128)(2,1)} %x_ref.3, ...), custom_call_target="tpu_custom_call" | custom-call | flops 6000000000 | bytes 6000000 | tf_op jit(solution)/shard_map/rates_forward/pallas_call | solution.py:854
  12.8 38.1 %mixer_forward.1 = (bf16[8,264,640]{2,1,0:T(8,128)(2,1)}, f32[256,1024]{1,0:T(8,128)}, f32[256,1024]{1,0:T(8,128)}, bf16[8,256,128]{2,1,0:T(8,128)(2,1)}, bf16[8...) custom-call(bf16[264,1024]{1,0:T(8,128)(2,1)} %get-tuple-element.98., ...), custom_call_target="tpu_custom_call" | custom-call | flops 40000000000 | bytes 40000000 | tf_op jit(solution)/shard_map/mixer_forward/pallas_call | solution.py:361
  50.9 62.6 %middle.1 = (bf16[256,1024]{1,0:T(8,128)(2,1)}, f32[256,1024]{1,0:T(8,128)}, bf16[8,128,128]{2,1,0:T(8,128)(2,1)}, f32[256,1024]{1,0:T(8,128)}, f32[1,1024]{1,0:...) custom-call(f32[256,1024]{1,0:T(8,128)} %get-tuple-element.109.refs_, ...), custom_call_target="tpu_custom_call" | custom-call | flops 30000001024 | bytes 30000000 | tf_op jit(solution)/shard_map/middle/pallas_call | solution.py:1173
  113.5 1.2 collective-permute-start
  114.7 0.0 collective-permute-start.1
  114.7 0.0 collective-permute-start.2
  114.7 27.8 %mixer_backward.1 = (bf16[264,5120]{1,0:T(8,128)(2,1)}, f32[4,1024]{1,0:T(4,128)}, f32[4,2048]{1,0:T(4,128)}, f32[4,2048]{1,0:T(4,128)}, f32[8,4,128,8]{3,2,1,0:T(8,128)}) custom-call(bf16[8,264,640]{2,1,0:T(8,128)(2,1)} %get-tuple-element.102.pre_ref, f32[4,1024]{1,0:T(4,128)} %tq_ref.3, f32[4,2048]{1,0:T(4,128)} %tk_ref.3, f32[4,2048]{1,0:T(4,128)} %tv_ref.3, ...), custom_call_target="tpu_custom_call" | custom-call | flops 35000000512 | bytes 35000000 | tf_op jit(solution)/shard_map/mixer_backward/pallas_call | solution.py:550
  142.5 13.3 %input_pull.1 = (bf16[256,1024]{1,0:T(8,128)(2,1)}, f32[3,8,1024]{2,1,0:T(8,128)}, f32[8,1024]{1,0:T(8,128)}, f32[1,1024]{1,0:T(1,128)}, f32[24,1024]{1,0:T(8,128)}, /*index=5*/f32[1,128]{1,0:T(1,128)}) custom-call(bf16[264,5120]{1,0:T(8,128)(2,1)} %get-tuple-element.115.d_ref.rhs_ref, bf16[256,1024]{1,0:T(8,128)(2,1)} %get-tuple-element.116.dg_ref, ...), custom_call_target="tpu_custom_call" | custom-call | flops 12000000000 | bytes 12000000 | tf_op jit(solution)/shard_map/input_pull/pallas_call | solution.py:714
  155.8 0.0 collective-permute-done.arr_a
  155.8 0.0 copy-start
  155.8 0.0 collective-permute-done.1.arr_b
  155.8 0.0 copy-start.1
  155.8 0.0 collective-permute-done.2.arr_c
  155.8 0.0 copy-start.2
  155.8 1.2 copy-done
  157.0 0.6 copy-done.1
  157.7 0.5 copy-done.2
  158.1 99.5 %reduce_all.1 = (f32[32,2816]{1,0:T(8,128)}, f32[32,2816]{1,0:T(8,128)}, f32[32,2816]{1,0:T(8,128)}, f32[32,1024]{1,0:T(8,128)}, f32[32,1024]{1,0:T(8,128)}, /*i...) custom-call(bf16[7,256,512]{2,1,0:T(8,128)(2,1)} %copy-done, ...), custom_call_target="tpu_custom_call" | custom-call | flops 89999998976 | bytes 90000000 | tf_op jit(solution)/shard_map/reduce_all/pallas_call | solution.py:1454
  257.6 3.7 %finish.1 = (bf16[256,1024]{1,0:T(8,128)(2,1)}, bf16[256,1024]{1,0:T(8,128)(2,1)}, f32[32,1024]{1,0:T(8,128)}, f32[32,2048]{1,0:T(8,128)}, f32[32,2048]{1,0:T(8,...) custom-call(bf16[256,1024]{1,0:T(8,128)(2,1)} %get-tuple-element.123, ...), custom_call_target="tpu_custom_call" | custom-call | flops 3000000000 | bytes 3000000 | tf_op jit(solution)/shard_map/finish/pallas_call | solution.py:1496
Async XLA Ops:
  113.5 42.3 %collective-permute-start = (bf16[7,256,512]{2,1,0:T(8,128)(2,1)}, bf16[7,256,512]{2,1,0:T(8,128)(2,1)S(1)}, u32[]{:S(2)}, u32[]{:S(2)}) collective-permute-start(bf16[7,256,512]{2,1,0:T(8,128)(2,1)} %get-tuple-element.124), channel_id=1, source_target_pairs={{0,1},{1,0},{2,3},{3,2},{4,5},{5,4},{6,7},{7,6},{8,9},{9,8},{10,11... | collective-permute-start | bytes 5505032 | tf_op jit(solution)/shard_map/ppermute | solution.py:1552
  114.7 41.1 %collective-permute-start.1 = (bf16[7,256,512]{2,1,0:T(8,128)(2,1)}, bf16[7,256,512]{2,1,0:T(8,128)(2,1)S(1)}, u32[]{:S(2)}, u32[]{:S(2)}) collective-permute-start(bf16[7,256,512]{2,1,0:T(8,128)(2,1)} %get-tuple-element.125), channel_id=1, source_target_pairs={{0,2},{1,3},{2,0},{3,1},{4,6},{5,7},{6,4},{7,5},{8,10},{9,11},{10,... | collective-permute-start | bytes 5505032 | tf_op jit(solution)/shard_map/ppermute | solution.py:1552
  114.7 41.1 %collective-permute-start.2 = (bf16[7,256,512]{2,1,0:T(8,128)(2,1)}, bf16[7,256,512]{2,1,0:T(8,128)(2,1)S(1)}, u32[]{:S(2)}, u32[]{:S(2)}) collective-permute-start(bf16[7,256,512]{2,1,0:T(8,128)(2,1)} %get-tuple-element.126), channel_id=1, source_target_pairs={{0,4},{1,5},{2,6},{3,7},{4,0},{5,1},{6,2},{7,3},{8,12},{9,13},{10,... | collective-permute-start | bytes 5505032 | tf_op jit(solution)/shard_map/ppermute | solution.py:1552
  155.8 1.2 copy-start
  155.8 1.9 copy-start.1
  155.8 2.3 copy-start.2
